TPU v7x, 128 devices: a whole 4x4x4 slice. The times are simulated.
128 devices in a mesh: corr: 4 (over x), tile: 32 (over z, y, core).
Axes of the slice: x: 4, y: 4, z: 4, core: 2. Of those that a mesh axis runs over, the one named last changes fastest.
Arguments:
- visibilities: bfloat16 [8192, 8, 256], P(('corr', 'tile')), may hold values from -6 to 6
- coords: float32 [8192, 3, 256], P(('corr', 'tile')), may hold values from -12 to 12
- stations: int32 [8192, 2], P(('corr', 'tile')), may hold values from 0 to 511
- tile_ids: int32 [8192, 1], P(('corr', 'tile')), may hold values from 0 to 63; in each aligned block of 64 rows (0 to 63, 64 to 127, ...) at most 2 rows name the same one
- offsets: int32 [8192, 2], P(('corr', 'tile')), may hold values from 0 to 96
- screens: bfloat16 [512, 8, 1024], P('tile'), may hold values from -4 to 4
Outputs:
- grid_tiles: float32 [4, 64, 2, 128, 128], P('corr', 'tile')
Inputs may be any that keep to these rules, and one draw needn't show every extreme that they name: `tile_ids`: within the rows of one device (aligned blocks of 64 rows) no uv-tile is named more than 2 times, and some uv-tile exactly 2 times.
All inputs are finite; a program needn't handle non-finite values.
Results may differ from a plain program's by a relative error of at most 0.0061.
Values may be sent and summed in bfloat16 or wider, within the bound.
A program may use at most 64 MiB of HBM per device.

v0:
```python
import functools
import math

import jax
import jax.numpy as jnp
import numpy as np
from jax import lax
from jax.experimental import pallas as pl
from jax.experimental.pallas import tpu as pltpu
from jax.sharding import PartitionSpec as P

SUB = 32
NT = 64
TILE_SIDE = 128
NVIS = 256
PIX = 1024
NCORR = 4
CAP = 2
NJ = 8
LANES = 128
SIN_POLY = (3.141592579805584, -5.167706866167941, 2.550031193519298, -0.5980441939119835, 0.07721838615698538)
COS_POLY = (0.9999999532476082, -4.934792830619647, 4.058411352862557, -1.3318765680805114, 0.2196896110968953)
ROOT_HALF = math.sqrt(0.5)
VMEM_LIMIT = 60 * 1024 * 1024


def uv_tables():
    rr = np.arange(4)[:, None, None, None]
    c = np.arange(SUB)[None, :, None, None]
    a4 = np.arange(4)[None, None, :, None]
    d = np.arange(SUB)[None, None, None, :]
    half = SUB // 2
    tables = []
    for a8 in range(NJ):
        turns = (rr * (a8 + 8 * a4 - half) + (c - half) * (d - half)) % SUB
        angle = (-2.0 * np.pi / SUB) * turns.reshape(LANES, LANES)
        re, im = np.cos(angle) / SUB, np.sin(angle) / SUB
        tables.append(np.block([[re, im], [-im, re]]))
    return jnp.asarray(np.stack(tables), jnp.bfloat16)


def taper_table():
    pos = (np.arange(SUB) - SUB // 2 + 0.5) / (SUB // 2)
    edge = 1.0 - 0.8 * pos * pos
    return jnp.asarray((edge[:, None] * edge[None, :] / NVIS).reshape(NJ, LANES), jnp.float32)


def poly(square, coefficients):
    total = jnp.full_like(square, coefficients[-1])
    for coefficient in coefficients[-2::-1]:
        total = total * square + coefficient
    return total


def cos_sin_turns(turns):
    rest = turns - jnp.round(turns)
    square = rest * rest
    sine = rest * poly(square, SIN_POLY)
    cosine = poly(square, COS_POLY)
    twice = sine + sine
    return 1.0 - twice * sine, twice * cosine


def direction_tables():
    row = lax.broadcasted_iota(jnp.int32, (2 * SUB, NVIS), 0)
    r = (row % NJ) * 4 + row // NJ
    place = jnp.where(row < SUB, r, row - SUB)
    first = (place - SUB // 2).astype(jnp.float32) * (1.0 / SUB)
    return first, -0.5 * first * first


def image_of(coords, vis, first, second):
    u, v, w = coords[0:1], coords[1:2], coords[2:3]
    linear = jnp.concatenate([u * first[:SUB], v * first[SUB:]], axis=0)
    cosine, sine = cos_sin_turns(linear + w * second)
    row_re, row_im = cosine[:SUB], sine[:SUB]
    col_re, col_im = cosine[SUB:], sine[SUB:]
    vis = vis.astype(jnp.float32)
    lhs = []
    for rr in range(4):
        a_re, a_im = row_re[rr * NJ:(rr + 1) * NJ], row_im[rr * NJ:(rr + 1) * NJ]
        part_re, part_im = [], []
        for e in range(NCORR):
            v_re, v_im = vis[e:e + 1], vis[NCORR + e:NCORR + e + 1]
            part_re.append(v_re * a_re - v_im * a_im)
            part_im.append(v_re * a_im + v_im * a_re)
        lhs.append(jnp.concatenate([jnp.concatenate(part_re, axis=0), jnp.concatenate(part_im, axis=0)], axis=1))
    lhs = jnp.concatenate(lhs, axis=0).astype(jnp.bfloat16)
    upper = jnp.concatenate([col_re, -col_im], axis=1)
    lower = jnp.concatenate([col_im, col_re], axis=1)
    rhs = jnp.concatenate([upper, lower, upper, lower], axis=0).astype(jnp.bfloat16)
    out = lax.dot_general(lhs, rhs, (((1,), (1,)), ((), ())), preferred_element_type=jnp.float32)
    parts = [out[rr * SUB:(rr + 1) * SUB] for rr in range(4)]
    turned = [pltpu.roll(part, SUB, 1) for part in parts]
    lane = lax.broadcasted_iota(jnp.int32, (SUB, LANES), 1)

    def join(a, b, c, d):
        return jnp.where(lane < SUB, a, jnp.where(lane < 2 * SUB, b, jnp.where(lane < 3 * SUB, c, d)))

    image_re = join(parts[0], turned[1], parts[2], turned[3])
    image_im = join(turned[0], parts[1], turned[2], parts[3])
    return image_re, image_im


def images_kernel(vis_ref, coords_ref, out_ref):
    first, second = direction_tables()

    def step(s, carry):
        image_re, image_im = image_of(coords_ref[s], vis_ref[s], first, second)
        out_ref[s, 0:SUB] = image_re
        out_ref[s, SUB:2 * SUB] = image_im
        return carry

    lax.fori_loop(0, vis_ref.shape[0], step, 0, unroll=2)


def images(visibilities, coords):
    count = visibilities.shape[0]
    vmem = pl.BlockSpec(memory_space=pltpu.VMEM)
    return pl.pallas_call(
        images_kernel,
        out_shape=jax.ShapeDtypeStruct((count, 2 * SUB, LANES), jnp.float32),
        in_specs=[vmem, vmem],
        out_specs=vmem,
        compiler_params=pltpu.CompilerParams(vmem_limit_bytes=VMEM_LIMIT),
        cost_estimate=pl.CostEstimate(flops=count * 2 * 128 * 512 * 128, bytes_accessed=4 << 20, transcendentals=0),
        name="images",
    )(visibilities, coords)


def sandwich_of(image, near, far):
    def row(array, index):
        return array[index * NJ:(index + 1) * NJ]

    mid_re, mid_im = {}, {}
    for out_row in range(2):
        for inner in range(2):
            total_re = total_im = None
            for first in range(2):
                n_re, n_im = row(near, 2 * first + out_row), row(near, 4 + 2 * first + out_row)
                v_re, v_im = row(image, 2 * first + inner), row(image, 4 + 2 * first + inner)
                re = n_re * v_re + n_im * v_im
                im = n_re * v_im - n_im * v_re
                total_re = re if total_re is None else total_re + re
                total_im = im if total_im is None else total_im + im
            mid_re[out_row, inner], mid_im[out_row, inner] = total_re, total_im
    out_re, out_im = [], []
    for out_row in range(2):
        for out_col in range(2):
            total_re = total_im = None
            for inner in range(2):
                m_re, m_im = mid_re[out_row, inner], mid_im[out_row, inner]
                f_re, f_im = row(far, 2 * inner + out_col), row(far, 4 + 2 * inner + out_col)
                re = m_re * f_re - m_im * f_im
                im = m_re * f_im + m_im * f_re
                total_re = re if total_re is None else total_re + re
                total_im = im if total_im is None else total_im + im
            out_re.append(total_re)
            out_im.append(total_im)
    return out_re, out_im


def fft8(re, im):
    def add(x, y):
        return x[0] + y[0], x[1] + y[1]

    def sub(x, y):
        return x[0] - y[0], x[1] - y[1]

    def turn(x):
        return x[1], -x[0]

    def fft4(x):
        even_add, even_sub = add(x[0], x[2]), sub(x[0], x[2])
        odd_add, odd_sub = add(x[1], x[3]), turn(sub(x[1], x[3]))
        return [add(even_add, odd_add), add(even_sub, odd_sub), sub(even_add, odd_add), sub(even_sub, odd_sub)]

    x = list(zip(re, im))
    even, odd = fft4(x[0::2]), fft4(x[1::2])
    odd = [
        odd[0],
        ((odd[1][0] + odd[1][1]) * ROOT_HALF, (odd[1][1] - odd[1][0]) * ROOT_HALF),
        turn(odd[2]),
        ((odd[3][1] - odd[3][0]) * ROOT_HALF, (-odd[3][0] - odd[3][1]) * ROOT_HALF),
    ]
    out = [add(even[k], odd[k]) for k in range(4)] + [sub(even[k], odd[k]) for k in range(4)]
    return [(-o[0], -o[1]) if k % 2 else o for k, o in enumerate(out)]


def blocks_kernel(count, stations, tile_ids, offsets, image_ref, taper_ref, table_ref, screens, send_ref, meta_ref,
                  near_far, x_re, x_im, y_ref, u_re, u_im, used, sems):
    def fetch(s, which):
        return pltpu.make_async_copy(screens.at[stations[s, which]], near_far.at[s, which], sems.at[s, which])

    def start(s, carry):
        fetch(s, 0).start()
        fetch(s, 1).start()
        return carry

    lax.fori_loop(0, count, start, 0)

    def clear(i, carry):
        used[i] = 0
        return carry

    lax.fori_loop(0, NT, clear, 0)

    def clear_meta(i, carry):
        meta_ref[i] = -1
        return carry

    lax.fori_loop(0, NT * CAP, clear_meta, 0)
    taper = taper_ref[...]

    def sandwich(s, carry):
        fetch(s, 0).wait()
        fetch(s, 1).wait()
        near = near_far[s, 0].astype(jnp.float32)
        far = near_far[s, 1].astype(jnp.float32)
        out_re, out_im = sandwich_of(image_ref[s], near, far)
        for e in range(NCORR):
            rows = pl.ds(pl.multiple_of(s * SUB + e * NJ, NJ), NJ)
            x_re[rows] = out_re[e] * taper
            x_im[rows] = out_im[e] * taper
        return carry

    lax.fori_loop(0, count, sandwich, 0, unroll=2)

    chunk = 16

    def transform(i, carry):
        base = i * (chunk * NJ)
        re = [x_re[pl.ds(base + j, chunk, stride=NJ)] for j in range(NJ)]
        im = [x_im[pl.ds(base + j, chunk, stride=NJ)] for j in range(NJ)]
        rows = pl.ds(pl.multiple_of(i * chunk, chunk), chunk)
        for a8, (y_re, y_im) in enumerate(fft8(re, im)):
            y_ref[a8, rows, 0:LANES] = y_re.astype(jnp.bfloat16)
            y_ref[a8, rows, LANES:2 * LANES] = y_im.astype(jnp.bfloat16)
        return carry

    lax.fori_loop(0, count * NCORR // chunk, transform, 0)

    for a8 in range(NJ):
        out = jnp.dot(y_ref[a8], table_ref[a8], preferred_element_type=jnp.float32)
        u_re[pl.ds(a8, count * NCORR, stride=NJ)] = out[:, 0:LANES]
        u_im[pl.ds(a8, count * NCORR, stride=NJ)] = out[:, LANES:2 * LANES]

    def pack(s, carry):
        tile = tile_ids[s]
        rank = used[tile]
        used[tile] = rank + 1
        slot = tile * CAP + rank
        meta_ref[slot] = offsets[s, 0] * TILE_SIDE + offsets[s, 1]
        target = pl.ds(pl.multiple_of(slot * 2 * NJ, 2 * NJ), 2 * NJ)
        for e in range(NCORR):
            rows = pl.ds(pl.multiple_of(s * SUB + e * NJ, NJ), NJ)
            send_ref[e, target] = jnp.concatenate([u_re[rows], u_im[rows]], axis=0).astype(jnp.bfloat16)
        return carry

    lax.fori_loop(0, count, pack, 0, unroll=2)


def blocks(image, screens, stations, tile_ids, offsets):
    count = image.shape[0]
    vmem = pl.BlockSpec(memory_space=pltpu.VMEM)
    smem = pl.BlockSpec(memory_space=pltpu.SMEM)
    slots = NT * CAP
    points = count * NCORR
    return pl.pallas_call(
        functools.partial(blocks_kernel, count),
        out_shape=(
            jax.ShapeDtypeStruct((NCORR, slots * 2 * NJ, LANES), jnp.bfloat16),
            jax.ShapeDtypeStruct((slots,), jnp.int32),
        ),
        in_specs=[smem, smem, smem, vmem, vmem, vmem, pl.BlockSpec(memory_space=pl.ANY)],
        out_specs=(vmem, smem),
        scratch_shapes=[
            pltpu.VMEM((count, 2, 2 * SUB, LANES), jnp.bfloat16),
            pltpu.VMEM((points * NJ, LANES), jnp.float32),
            pltpu.VMEM((points * NJ, LANES), jnp.float32),
            pltpu.VMEM((NJ, points, 2 * LANES), jnp.bfloat16),
            pltpu.VMEM((points * NJ, LANES), jnp.float32),
            pltpu.VMEM((points * NJ, LANES), jnp.float32),
            pltpu.SMEM((NT,), jnp.int32),
            pltpu.SemaphoreType.DMA((count, 2)),
        ],
        compiler_params=pltpu.CompilerParams(vmem_limit_bytes=VMEM_LIMIT),
        name="blocks",
    )(stations, tile_ids, offsets, image, taper_table(), uv_tables(), screens)


def gather_kernel(sources, per_owner, meta, recv_ref, out_ref, acc):
    acc[...] = jnp.zeros_like(acc)
    lane = lax.broadcasted_iota(jnp.int32, (NJ, LANES), 1)
    slots = per_owner * CAP

    def step(src, carry):
        for slot in range(slots):
            place = meta[src * slots + slot]
            valid = place >= 0
            row0 = jnp.where(valid, place // TILE_SIDE, 0)
            col0 = jnp.where(valid, place % TILE_SIDE, 0)
            begin = jnp.where(valid, row0, 2 * LANES)
            inside = (lane >= begin) & (lane < begin + SUB)
            block = recv_ref[src, slot * 2 * NJ:(slot + 1) * 2 * NJ].astype(jnp.float32)
            for part in range(2):
                data = block[part * NJ:(part + 1) * NJ]
                for a4 in range(4):
                    shift = jnp.where(row0 >= a4 * SUB, row0 - a4 * SUB, row0 - a4 * SUB + LANES)
                    moved = jnp.where(inside, pltpu.roll(data, shift, 1), 0.0)
                    rows = pl.ds(col0 + NJ * a4, NJ)
                    acc[slot, part, rows] = acc[slot, part, rows] + moved
        return carry

    lax.fori_loop(0, sources, step, 0)
    for tile in range(per_owner):
        for part in range(2):
            total = acc[tile * CAP, part]
            for rank in range(1, CAP):
                total = total + acc[tile * CAP + rank, part]
            out_ref[tile, part] = total.T


def gather_blocks(received, meta, per_owner):
    sources = received.shape[0]
    vmem = pl.BlockSpec(memory_space=pltpu.VMEM)
    return pl.pallas_call(
        functools.partial(gather_kernel, sources, per_owner),
        out_shape=jax.ShapeDtypeStruct((per_owner, 2, TILE_SIDE, TILE_SIDE), jnp.float32),
        in_specs=[pl.BlockSpec(memory_space=pltpu.SMEM), vmem],
        out_specs=vmem,
        scratch_shapes=[pltpu.VMEM((per_owner * CAP, 2, TILE_SIDE, TILE_SIDE), jnp.float32)],
        compiler_params=pltpu.CompilerParams(vmem_limit_bytes=VMEM_LIMIT),
        name="accumulate",
    )(meta, received)


def per_device(visibilities, coords, stations, tile_ids, offsets, screens):
    tile_size = lax.axis_size("tile")
    corr_size = lax.axis_size("corr")
    per_owner = NT // tile_size
    own = screens.reshape(screens.shape[0], 2 * SUB, LANES)
    all_screens = lax.all_gather(own, "tile", axis=0, tiled=True)
    image = images(visibilities, coords)
    sending, meta = blocks(image, all_screens, stations, tile_ids[:, 0], offsets)
    rows = per_owner * CAP * 2 * NJ
    received = lax.all_to_all(
        sending.reshape(NCORR * tile_size, rows, LANES), ("corr", "tile"), split_axis=0, concat_axis=0, tiled=True
    )
    meta = jnp.broadcast_to(meta.reshape(1, tile_size, per_owner * CAP), (corr_size, tile_size, per_owner * CAP))
    got_meta = lax.all_to_all(
        meta.reshape(corr_size * tile_size, per_owner * CAP), ("corr", "tile"), split_axis=0, concat_axis=0, tiled=True
    )
    return gather_blocks(received, got_meta.reshape(-1), per_owner)[None]


def solution(mesh):
    return jax.shard_map(
        per_device,
        mesh=mesh,
        in_specs=(
            P(("corr", "tile"), None, None),
            P(("corr", "tile"), None, None),
            P(("corr", "tile"), None),
            P(("corr", "tile"), None),
            P(("corr", "tile"), None),
            P("tile", None, None),
        ),
        out_specs=P("corr", "tile", None, None, None),
        check_vma=False,
    )
```

profile of v0, /device:TPU:1, one launch (start us, length us, event | category | flops | bytes accessed | tf_op | source)
XLA Modules:
  0.0 153.0 jit_solution(13119779148599026911)
XLA Ops:
  6.5 0.0 all-gather.2.cloned.1.call-start
  6.5 1.8 %reshape.16 = bf16[16,64,128]{2,1,0:T(8,128)(2,1)} reshape(bf16[16,8,1024]{2,1,0:T(8,128)(2,1)} %param.13) | data formatting | bytes 524288 | tf_op jit(solution)/shard_map/reshape | solution.py:342
  8.3 0.0 all-gather.2.cloned.1.call-update
  8.3 1.8 %copy.15.coords_ref = f32[64,3,256]{2,1,0:T(4,128)} copy(f32[64,3,256]{2,0,1:T(8,128)} %param.9) | data formatting | bytes 393216 | tf_op args[1]
  10.1 1.4 copy.16.stations
  11.5 1.4 copy.17.offsets
  12.9 16.3 %images.1.image_ref = f32[64,64,128]{2,1,0:T(8,128)} custom-call(bf16[64,8,256]{2,1,0:T(8,128)(2,1)} %vis_ref.1, f32[64,3,256]{2,1,0:T(4,128)} %copy.15.coords_ref), custom_call_target="tpu_custom_call" | custom-call | flops 1073741824 | bytes 4194304 | tf_op jit(solution)/shard_map/images/pallas_call | solution.py:120
  29.2 37.0 %all-gather.2.cloned.1.call-done.screens = bf16[512,64,128]{2,1,0:T(8,128)(2,1)} async-done(((bf16[16,64,128]{2,1,0:T(8,128)(2,1)}), bf16[512,64,128]{2,1,0:T(8,128)(2,1)}) %all-gather.2.cloned.1.call-update) | async-done | bytes 8388624 | tf_op jit(solution)/shard_map/all_gather | solution.py:343
  66.2 9.3 %blocks.1 = (bf16[4,2048,128]{2,1,0:T(8,128)(2,1)}, s32[128]{0:T(128)}) custom-call(s32[64,2]{1,0:T(8,128)} %copy.16.stations, s32[64]{0:T(128)} %bitcast.6, s32[64,2]{1,0:T(8,128)} %copy.17.offsets, f32[64,64,128]{2,1,0:T(8,128)} %images.1.image_ref, f32[8,128]{1,0:T(8,128)} %constant.4.clone.taper_ref, bf16[8,256,256]{2,1,0:T(8,128)(2,1)} %constant.5.clone.table_ref, ...), custom_call_target="tpu_custom_call" | custom-call | tf_op jit(solution)/shard_map/blocks/pallas_call | solution.py:269
  75.5 0.8 broadcast_in_dim.10
  76.2 16.7 %all_to_all.14 = s32[128,1,4]{2,1,0:T(1,128)S(1)} all-to-all(s32[128,1,4]{2,1,0:T(1,128)S(1)} %bitcast.5), channel_id=1, replica_groups=mesh['corr'=4,'tile'=32] {'corr','tile'}, dimensions={0} | all-to-all | bytes 4096 | tf_op jit(solution)/shard_map/all_to_all | solution.py:351
  92.9 4.6 %all-to-all-start.1 = ((bf16[128,64,128]{2,1,0:T(8,128)(2,1)}), bf16[128,64,128]{2,1,0:T(8,128)(2,1)S(1)}, u32[]{:S(2)}, u32[]{:S(2)}) async-start(bf16[128,64,128]{2,1,0:T(8,128)(2,1)} %bitcast.4), calls=%async_computation.1 | async-start | bytes 4194304 | tf_op jit(solution)/shard_map/all_to_all | solution.py:347
  97.6 0.5 broadcast.3
  98.1 0.8 reduce.3
  98.9 0.7 reshape.17.meta
  99.6 28.2 %all-to-all-done.1.recv_ref = bf16[128,64,128]{2,1,0:T(8,128)(2,1)S(1)} async-done(((bf16[128,64,128]{2,1,0:T(8,128)(2,1)}), bf16[128,64,128]{2,1,0:T(8,128)(2,1)S(1)}, u32[]{:S(2)}, u32[]{:S(2)}) %all-to-all-start.1) | async-done | bytes 2097184 | tf_op jit(solution)/shard_map/all_to_all | solution.py:347
  127.8 0.0 copy-start
  127.8 1.3 copy-done
  129.1 17.1 %accumulate.1 = f32[2,2,128,128]{3,2,1,0:T(8,128)} custom-call(s32[512]{0:T(512)} %reshape.17.meta, bf16[128,64,128]{2,1,0:T(8,128)(2,1)} %copy-done), custom_call_target="tpu_custom_call" | custom-call | tf_op jit(solution)/shard_map/accumulate/pallas_call | solution.py:327
  (1 shorter events, 0.0 us)
Async XLA Ops:
  6.5 59.6 %all-gather.2.cloned.1.call-start = ((), (), s32[]{:S(2)}) async-start(), calls=%async_computation.2 | async-start | bytes 8650752 | tf_op jit(solution)/shard_map/all_gather | solution.py:343
  92.9 34.8 %all-to-all-start.1 = ((bf16[128,64,128]{2,1,0:T(8,128)(2,1)}), bf16[128,64,128]{2,1,0:T(8,128)(2,1)S(1)}, u32[]{:S(2)}, u32[]{:S(2)}) async-start(bf16[128,64,128]{2,1,0:T(8,128)(2,1)} %bitcast.4), calls=%async_computation.1 | async-start | bytes 4194304 | tf_op jit(solution)/shard_map/all_to_all | solution.py:347
  127.8 1.3 copy-start
Sparse Core Ops, SparseCore 0:
  9.6 56.5 all-gather.1
where the time goes:
time: 153 us
  waiting for transfers between devices  65.2 us (43%)
  Pallas kernels  42.7 us (28%)
  blocking collectives  16.7 us (11%)
  between operations  13.4 us (9%)
  local copies, waits for them, and re-layouts  9.58 us (6%)
  starting transfers between devices  4.62 us (3%)
    all_gather x1, waiting for transfers between devices, per_device(): all_screens = lax.all_gather(own, 'tile', axis=0, tiled=True)  37 us
    all_to_all x1, waiting for transfers between devices, per_device(): lax.all_to_all(sending.reshape(NCORR * tile_size, rows, LANES), ('corr',...  28.2 us
    pallas_call x1, Pallas kernels, gather_blocks(): pl.pallas_call(functools.partial(gather_kernel, sources, per_owner), out_...  17.1 us
    all_to_all x1, blocking collectives, per_device(): lax.all_to_all(meta.reshape(corr_size * tile_size, per_owner * CAP), ('co...  16.7 us
    pallas_call x1, Pallas kernels, images(): pl.pallas_call(images_kernel, out_shape=jax.ShapeDtypeStruct((count, 2 *...  16.3 us
    pallas_call x1, Pallas kernels, blocks(): pl.pallas_call(functools.partial(blocks_kernel, count), out_shape=(jax.Sh...  9.29 us
    unnamed x5, local copies, waits for them, and re-layouts  5.86 us
    all_to_all x1, starting transfers between devices, per_device(): lax.all_to_all(sending.reshape(NCORR * tile_size, rows, LANES), ('corr',...  4.62 us
  transfers between devices with their start and end apart: 2, of which 2 were waited for; matrix products, arithmetic and copies ran while one was open for 4% of the time, Pallas kernels for 11%

commit v1 on v0

--- a/solution.py
+++ b/solution.py
@@ -102,30 +102,172 @@
     return image_re, image_im
 
 
-def images_kernel(vis_ref, coords_ref, out_ref):
+def ring_plan():
+    return (
+        ((3, 0, 0), (1, 0, 1)),
+        ((3, 0, 1), (1, 0, 0)),
+        ((0, 3, 0), (0, 1, 1)),
+        ((0, 3, 1), (0, 1, 0)),
+        ((2, 0, 0), (2, 0, 1)),
+        ((3, 3, 0), (3, 1, 1), (1, 3, 0), (1, 1, 1)),
+        ((0, 2, 0), (0, 2, 1)),
+        ((3, 3, 1), (3, 1, 0), (1, 3, 1), (1, 1, 0)),
+        ((2, 3, 0), (2, 1, 1)),
+        ((3, 2, 0), (3, 2, 1), (1, 2, 0), (1, 2, 1)),
+        ((2, 3, 1), (2, 1, 0)),
+        ((2, 2, 0), (2, 2, 1)),
+    )
+
+
+def screens_kernel(per_chunk, waits, own_ref, vis_ref, coords_ref, all_ref, image_ref, send_sems, ring_sems, pair_sems,
+                   own_sem):
+    tile = lax.axis_index("tile")
+    core, y, z = tile % 2, tile // 2 % 4, tile // 8
+
+    def chip(who, a, b):
+        there_z = (z + who * a + (1 - who) * b) % 4
+        there_y = (y + (1 - who) * a + who * b) % 4
+        return (there_z * 4 + there_y) * 2 + who
+
+    first_up, first_down = chip(core, 1, 0), chip(core, 3, 0)
+    second_up, second_down = chip(core, 0, 1), chip(core, 0, 3)
+    pair = (z * 4 + y) * 2 + (1 - core)
+    targets = (first_up, first_down, second_up, second_down, pair)
+
+    barrier = pltpu.get_barrier_semaphore()
+    for target in targets:
+        pl.semaphore_signal(barrier, inc=1, device_id={"tile": target}, device_id_type=pl.DeviceIdType.MESH)
+    pl.semaphore_wait(barrier, len(targets))
+
+    half = own_ref.shape[0] // 2
+    sent = []
+
+    def place(owner, h):
+        return all_ref.at[pl.ds(pl.multiple_of(owner * (2 * half) + h * half, half), half)]
+
+    def unit_index(unit):
+        return (unit[0] * 4 + unit[1]) * 2 + unit[2]
+
+    def copy_of(unit, target, sem, number):
+        a, b, h = unit
+        owner = chip(core, a, b)
+        source = own_ref.at[pl.ds(h * half, half)] if (a, b) == (0, 0) else place(owner, h)
+        return pltpu.make_async_remote_copy(
+            src_ref=source, dst_ref=place(owner, h), send_sem=send_sems.at[number], recv_sem=sem,
+            device_id={"tile": target}, device_id_type=pl.DeviceIdType.MESH,
+        )
+
+    def push(unit, target, arrives):
+        sem = pair_sems.at[unit_index(unit)] if arrives is None else ring_sems.at[unit_index(arrives)]
+        copy_of(unit, target, sem, len(sent)).start()
+        sent.append(unit)
+
+    def await_ring(unit):
+        copy_of(unit, first_up, ring_sems.at[unit_index(unit)], 0).wait_recv()
+
+    def await_pair(unit):
+        a, b, h = unit
+        owner = chip(1 - core, a, b)
+        pltpu.make_async_remote_copy(
+            src_ref=place(owner, h), dst_ref=place(owner, h), send_sem=send_sems.at[0],
+            recv_sem=pair_sems.at[unit_index(unit)], device_id={"tile": pair}, device_id_type=pl.DeviceIdType.MESH,
+        ).wait_recv()
+
+    def forward(unit):
+        a, b, h = unit
+        if b == 0:
+            if (a, h) == (3, 0):
+                push(unit, first_up, (2, 0, 0))
+            if (a, h) == (1, 1):
+                push(unit, first_down, (2, 0, 1))
+            up, down = lambda: push(unit, second_up, (a, 3, h)), lambda: push(unit, second_down, (a, 1, h))
+            for go in (up, down) if h == 0 else (down, up):
+                go()
+        elif (b, h) == (3, 0):
+            push(unit, second_up, (a, 2, 0))
+        elif (b, h) == (1, 1):
+            push(unit, second_down, (a, 2, 1))
+        push(unit, pair, None)
+
+    push((0, 0, 0), first_up, (3, 0, 0))
+    push((0, 0, 1), first_down, (1, 0, 1))
+    push((0, 0, 1), first_up, (3, 0, 1))
+    push((0, 0, 0), first_down, (1, 0, 0))
+    push((0, 0, 0), second_up, (0, 3, 0))
+    push((0, 0, 1), second_down, (0, 1, 1))
+    push((0, 0, 1), second_up, (0, 3, 1))
+    push((0, 0, 0), second_down, (0, 1, 0))
+    for h in range(2):
+        push((0, 0, h), pair, None)
+    local = pltpu.make_async_copy(own_ref, all_ref.at[pl.ds(pl.multiple_of(tile * (2 * half), half), 2 * half)], own_sem)
+    local.start()
+
     first, second = direction_tables()
 
-    def step(s, carry):
-        image_re, image_im = image_of(coords_ref[s], vis_ref[s], first, second)
-        out_ref[s, 0:SUB] = image_re
-        out_ref[s, SUB:2 * SUB] = image_im
-        return carry
-
-    lax.fori_loop(0, vis_ref.shape[0], step, 0, unroll=2)
-
-
-def images(visibilities, coords):
+    def compute(begin, end):
+        def step(s, carry):
+            image_re, image_im = image_of(coords_ref[s], vis_ref[s], first, second)
+            image_ref[s, 0:SUB] = image_re
+            image_ref[s, SUB:2 * SUB] = image_im
+            return carry
+
+        lax.fori_loop(begin, end, step, 0)
+
+    groups = ring_plan()
+    count = vis_ref.shape[0]
+    chunks = count // per_chunk
+
+    def chunk(i, carry):
+        compute(i * per_chunk, (i + 1) * per_chunk)
+        for group, when in zip(groups, waits):
+            if when is not None:
+                @pl.when(i == when)
+                def _():
+                    for unit in group:
+                        await_ring(unit)
+                        forward(unit)
+        return carry
+
+    lax.fori_loop(0, chunks, chunk, 0)
+    for group, when in zip(groups, waits):
+        if when is None:
+            for unit in group:
+                await_ring(unit)
+                forward(unit)
+    for a in range(4):
+        for b in range(4):
+            for h in range(2):
+                await_pair((a, b, h))
+    for number, unit in enumerate(sent):
+        copy_of(unit, pair, pair_sems.at[0], number).wait_send()
+    local.wait()
+
+
+WAITS = (3, 4, 5, 6, 7, 9, 11, 13, None, None, None, None)
+
+
+def gather_screens(own, visibilities, coords, tile_size):
     count = visibilities.shape[0]
     vmem = pl.BlockSpec(memory_space=pltpu.VMEM)
+    own_count = own.shape[0]
+    copies = 62
     return pl.pallas_call(
-        images_kernel,
-        out_shape=jax.ShapeDtypeStruct((count, 2 * SUB, LANES), jnp.float32),
-        in_specs=[vmem, vmem],
-        out_specs=vmem,
-        compiler_params=pltpu.CompilerParams(vmem_limit_bytes=VMEM_LIMIT),
-        cost_estimate=pl.CostEstimate(flops=count * 2 * 128 * 512 * 128, bytes_accessed=4 << 20, transcendentals=0),
-        name="images",
-    )(visibilities, coords)
+        functools.partial(screens_kernel, 4, WAITS),
+        out_shape=(
+            jax.ShapeDtypeStruct((own_count * tile_size,) + own.shape[1:], own.dtype),
+            jax.ShapeDtypeStruct((count, 2 * SUB, LANES), jnp.float32),
+        ),
+        in_specs=[vmem, vmem, vmem],
+        out_specs=(pl.BlockSpec(memory_space=pl.ANY), vmem),
+        scratch_shapes=[
+            pltpu.SemaphoreType.DMA((copies,)),
+            pltpu.SemaphoreType.DMA((32,)),
+            pltpu.SemaphoreType.DMA((32,)),
+            pltpu.SemaphoreType.DMA,
+        ],
+        compiler_params=pltpu.CompilerParams(vmem_limit_bytes=VMEM_LIMIT, collective_id=0, has_side_effects=True),
+        name="screens",
+    )(own, visibilities, coords)
 
 
 def sandwich_of(image, near, far):
@@ -289,30 +431,123 @@
     )(stations, tile_ids, offsets, image, taper_table(), uv_tables(), screens)
 
 
-def gather_kernel(sources, per_owner, meta, recv_ref, out_ref, acc):
+def exchange_kernel(send_ref, meta_ref, recv_ref, table_ref, data_out, data_in, meta_out, meta_in, own_sem, stage):
+    corr, tile = lax.axis_index("corr"), lax.axis_index("tile")
+    core, y, z = tile % 2, tile // 2 % 4, tile // 8
+    devices = recv_ref.shape[0]
+    me = corr * (devices // 4) + tile
+
+    def there(k, sign):
+        x1 = (corr + sign * (k // 32 % 4) + 4) % 4
+        z1 = (z + sign * (k // 8 % 4) + 4) % 4
+        y1 = (y + sign * (k // 2 % 4) + 4) % 4
+        c1 = (core + k) % 2
+        return x1, (z1 * 4 + y1) * 2 + c1
+
+    def device(k):
+        x1, t1 = there(k, 1)
+        return {"corr": x1, "tile": t1}
+
+    barrier = pltpu.get_barrier_semaphore()
+
+    def greet(k, carry):
+        pl.semaphore_signal(barrier, inc=1, device_id=device(k), device_id_type=pl.DeviceIdType.MESH)
+        return carry
+
+    lax.fori_loop(1, devices, greet, 0)
+    take = pltpu.make_async_copy(send_ref.at[me], stage, own_sem)
+    take.start()
+    take.wait()
+    put = pltpu.make_async_copy(stage, recv_ref.at[me], own_sem)
+    put.start()
+    put.wait()
+    put = pltpu.make_async_copy(meta_ref.at[0], table_ref.at[me], own_sem)
+    put.start()
+    put.wait()
+    pl.semaphore_wait(barrier, devices - 1)
+
+    def data_copy(k):
+        x1, t1 = there(k, 1)
+        return pltpu.make_async_remote_copy(
+            src_ref=send_ref.at[x1 * (devices // 4) + t1], dst_ref=recv_ref.at[me],
+            send_sem=data_out.at[k], recv_sem=data_in.at[k],
+            device_id={"corr": x1, "tile": t1}, device_id_type=pl.DeviceIdType.MESH,
+        )
+
+    def meta_copy(k):
+        return pltpu.make_async_remote_copy(
+            src_ref=meta_ref.at[0], dst_ref=table_ref.at[me],
+            send_sem=meta_out.at[k], recv_sem=meta_in.at[k], device_id=device(k), device_id_type=pl.DeviceIdType.MESH,
+        )
+
+    def start(k, carry):
+        meta_copy(k).start()
+        data_copy(k).start()
+        return carry
+
+    lax.fori_loop(1, devices, start, 0)
+
+    def finish(k, carry):
+        x1, t1 = there(k, -1)
+        source = x1 * (devices // 4) + t1
+        pltpu.make_async_remote_copy(
+            src_ref=send_ref.at[source], dst_ref=recv_ref.at[source], send_sem=data_out.at[k], recv_sem=data_in.at[k],
+            device_id={"corr": x1, "tile": t1}, device_id_type=pl.DeviceIdType.MESH,
+        ).wait()
+        pltpu.make_async_remote_copy(
+            src_ref=meta_ref.at[0], dst_ref=table_ref.at[source], send_sem=meta_out.at[k], recv_sem=meta_in.at[k],
+            device_id={"corr": x1, "tile": t1}, device_id_type=pl.DeviceIdType.MESH,
+        ).wait()
+        return carry
+
+    lax.fori_loop(1, devices, finish, 0)
+
+
+def exchange(sending, meta):
+    devices = sending.shape[0]
+    hbm = pl.BlockSpec(memory_space=pl.ANY)
+    vmem = pl.BlockSpec(memory_space=pltpu.VMEM)
+    sems = pltpu.SemaphoreType.DMA((devices,))
+    return pl.pallas_call(
+        exchange_kernel,
+        out_shape=(
+            jax.ShapeDtypeStruct(sending.shape, sending.dtype),
+            jax.ShapeDtypeStruct((devices,) + meta.shape[1:], meta.dtype),
+        ),
+        in_specs=[hbm, vmem],
+        out_specs=(hbm, vmem),
+        scratch_shapes=[sems, sems, sems, sems, pltpu.SemaphoreType.DMA, pltpu.VMEM(sending.shape[1:], sending.dtype)],
+        compiler_params=pltpu.CompilerParams(vmem_limit_bytes=VMEM_LIMIT, collective_id=1, has_side_effects=True),
+        name="exchange",
+    )(sending, meta)
+
+
+def gather_kernel(sources, per_owner, table, recv_ref, out_ref, acc):
     acc[...] = jnp.zeros_like(acc)
     lane = lax.broadcasted_iota(jnp.int32, (NJ, LANES), 1)
     slots = per_owner * CAP
+    own = lax.axis_index("tile") * slots
 
     def step(src, carry):
         for slot in range(slots):
-            place = meta[src * slots + slot]
+            place = table[src, own + slot]
             valid = place >= 0
-            row0 = jnp.where(valid, place // TILE_SIDE, 0)
-            col0 = jnp.where(valid, place % TILE_SIDE, 0)
+            row0 = jnp.where(valid, place >> 7, 0)
+            col0 = jnp.where(valid, place & (TILE_SIDE - 1), 0)
             begin = jnp.where(valid, row0, 2 * LANES)
             inside = (lane >= begin) & (lane < begin + SUB)
             block = recv_ref[src, slot * 2 * NJ:(slot + 1) * 2 * NJ].astype(jnp.float32)
             for part in range(2):
                 data = block[part * NJ:(part + 1) * NJ]
+                moved = []
                 for a4 in range(4):
-                    shift = jnp.where(row0 >= a4 * SUB, row0 - a4 * SUB, row0 - a4 * SUB + LANES)
-                    moved = jnp.where(inside, pltpu.roll(data, shift, 1), 0.0)
-                    rows = pl.ds(col0 + NJ * a4, NJ)
-                    acc[slot, part, rows] = acc[slot, part, rows] + moved
-        return carry
-
-    lax.fori_loop(0, sources, step, 0)
+                    shift = (row0 + (LANES - a4 * SUB)) & (LANES - 1)
+                    moved.append(jnp.where(inside, pltpu.roll(data, shift, 1), 0.0))
+                rows = pl.ds(col0, SUB)
+                acc[slot, part, rows] = acc[slot, part, rows] + jnp.concatenate(moved, axis=0)
+        return carry
+
+    lax.fori_loop(0, sources, step, 0, unroll=2)
     for tile in range(per_owner):
         for part in range(2):
             total = acc[tile * CAP, part]
@@ -337,21 +572,13 @@
 
 def per_device(visibilities, coords, stations, tile_ids, offsets, screens):
     tile_size = lax.axis_size("tile")
-    corr_size = lax.axis_size("corr")
     per_owner = NT // tile_size
     own = screens.reshape(screens.shape[0], 2 * SUB, LANES)
-    all_screens = lax.all_gather(own, "tile", axis=0, tiled=True)
-    image = images(visibilities, coords)
+    all_screens, image = gather_screens(own, visibilities, coords, tile_size)
     sending, meta = blocks(image, all_screens, stations, tile_ids[:, 0], offsets)
     rows = per_owner * CAP * 2 * NJ
-    received = lax.all_to_all(
-        sending.reshape(NCORR * tile_size, rows, LANES), ("corr", "tile"), split_axis=0, concat_axis=0, tiled=True
-    )
-    meta = jnp.broadcast_to(meta.reshape(1, tile_size, per_owner * CAP), (corr_size, tile_size, per_owner * CAP))
-    got_meta = lax.all_to_all(
-        meta.reshape(corr_size * tile_size, per_owner * CAP), ("corr", "tile"), split_axis=0, concat_axis=0, tiled=True
-    )
-    return gather_blocks(received, got_meta.reshape(-1), per_owner)[None]
+    received, table = exchange(sending.reshape(NCORR * tile_size, rows, LANES), meta.reshape(1, 1, NT * CAP))
+    return gather_blocks(received, table.reshape(-1, NT * CAP), per_owner)[None]
 
 
 def solution(mesh):

time: 153 us -> 115 us (0.75)
  Pallas kernels: 42.7 us -> 108 us
  waiting for transfers between devices: 65.2 us -> 0 us
  blocking collectives: 16.7 us -> 0 us
  between operations: 13.4 us -> 0.03 us
  starting transfers between devices: 4.62 us -> 0 us
  local copies, waits for them, and re-layouts: 9.58 us -> 6.31 us
    pallas_call x1 -> x2, Pallas kernels: 16.3 us -> 88 us  [the longest x1 48.7 us: exchange(): pl.pallas_call(exchange_kernel, out_shape=(jax.ShapeDtypeStruct(sending.s...]
    all_gather x1 -> x0, waiting for transfers between devices: 37 us -> none  [per_device(): all_screens = lax.all_gather(own, 'tile', axis=0, tiled=True)]
    all_to_all x1 -> x0, waiting for transfers between devices: 28.2 us -> none  [per_device(): lax.all_to_all(sending.reshape(NCORR * tile_size, rows, LANES), ('corr',...]
    all_to_all x1 -> x0, blocking collectives: 16.7 us -> none  [per_device(): lax.all_to_all(meta.reshape(corr_size * tile_size, per_owner * CAP), ('co...]
    pallas_call x1, Pallas kernels: 17.1 us -> 10.6 us  [gather_blocks(): pl.pallas_call(functools.partial(gather_kernel, sources, per_owner), out_...]
    all_to_all x1 -> x0, starting transfers between devices: 4.62 us -> none  [per_device(): lax.all_to_all(sending.reshape(NCORR * tile_size, rows, LANES), ('corr',...]
    unnamed x5 -> x3, local copies, waits for them, and re-layouts: 5.86 us -> 4.55 us
  transfers between devices with their start and end apart: 2 -> 0, of which waited for: 2 -> 0; matrix products, arithmetic and copies ran while one was open for 4% -> 0% of each run, Pallas kernels for 11% -> 0%
where the time goes in v1:
time: 115 us; the launch traced here: 114 us
  Pallas kernels  108 us (94%)
  local copies, waits for them, and re-layouts  6.31 us (5%)
    pallas_call x1, Pallas kernels, exchange(): pl.pallas_call(exchange_kernel, out_shape=(jax.ShapeDtypeStruct(sending.s...  48.7 us
    pallas_call x1, Pallas kernels, gather_screens(): pl.pallas_call(functools.partial(screens_kernel, 4, WAITS), out_shape=(ja...  39.3 us
    pallas_call x1, Pallas kernels, gather_blocks(): pl.pallas_call(functools.partial(gather_kernel, sources, per_owner), out_...  10.6 us
    pallas_call x1, Pallas kernels, blocks(): pl.pallas_call(functools.partial(blocks_kernel, count), out_shape=(jax.Sh...  9.36 us
    unnamed x3, local copies, waits for them, and re-layouts  4.55 us

profile of v1, /device:TPU:1, one launch (start us, length us, event | category | flops | bytes accessed | tf_op | source)
XLA Modules:
  0.0 114.2 jit_solution(1652176812330602213)
XLA Ops:
  0.0 1.4 %copy.10.stations = s32[64,2]{1,0:T(8,128)} copy(s32[64,2]{0,1:T(2,128)} %param.10) | data formatting | bytes 1024 | tf_op args[2]
  1.4 1.4 %copy.11.offsets = s32[64,2]{1,0:T(8,128)} copy(s32[64,2]{0,1:T(2,128)} %param.12) | data formatting | bytes 1024 | tf_op args[4]
  2.8 1.8 %copy.9.coords_ref = f32[64,3,256]{2,1,0:T(4,128)} copy(f32[64,3,256]{2,0,1:T(8,128)} %param.9) | data formatting | bytes 393216 | tf_op args[1]
  4.5 1.8 %reshape.12.own_ref = bf16[16,64,128]{2,1,0:T(8,128)(2,1)} reshape(bf16[16,8,1024]{2,1,0:T(8,128)(2,1)} %param.13) | data formatting | bytes 524288 | tf_op jit(solution)/shard_map/reshape | solution.py:576
  6.3 39.3 %screens.1 = (bf16[512,64,128]{2,1,0:T(8,128)(2,1)}, f32[64,64,128]{2,1,0:T(8,128)}) custom-call(bf16[16,64,128]{2,1,0:T(8,128)(2,1)} %reshape.12.own_ref, bf16[64,8,256]{2,1,0:T(8,128)(2,1)} %vis_ref.1, f32[64,3,256]{2,1,0:T(4,128)} %copy.9.coords_ref), custom_call_target="tpu_custom_call" | custom-call | tf_op jit(solution)/shard_map/screens/pallas_call | solution.py:254
  45.6 9.4 %blocks.1 = (bf16[4,2048,128]{2,1,0:T(8,128)(2,1)}, s32[128]{0:T(128)}) custom-call(s32[64,2]{1,0:T(8,128)} %copy.10.stations, s32[64]{0:T(128)} %bitcast.7, s32[64,2]{1,0:T(8,128)} %copy.11.offsets, f32[64,64,128]{2,1,0:T(8,128)} %get-tuple-element.11.image_ref, f32[8,128]{1,0:T(8,128)} %constant.4.clone.taper_ref, ...), custom_call_target="tpu_custom_call" | custom-call | tf_op jit(solution)/shard_map/blocks/pallas_call | solution.py:411
  55.0 48.7 %exchange.1 = (bf16[128,64,128]{2,1,0:T(8,128)(2,1)}, s32[128,1,128]{2,1,0:T(1,128)}) custom-call(bf16[128,64,128]{2,1,0:T(8,128)(2,1)} %bitcast.5, s32[1,1,128]{2,1,0:T(1,128)} %bitcast.8), custom_call_target="tpu_custom_call" | custom-call | tf_op jit(solution)/shard_map/exchange/pallas_call | solution.py:511
  103.7 10.6 %accumulate.1 = f32[2,2,128,128]{3,2,1,0:T(8,128)} custom-call(s32[128,128]{1,0:T(8,128)} %bitcast.6, bf16[128,64,128]{2,1,0:T(8,128)(2,1)} %get-tuple-element.16.recv_ref), custom_call_target="tpu_custom_call" | custom-call | tf_op jit(solution)/shard_map/accumulate/pallas_call | solution.py:562

commit v2 on v1

--- a/solution.py
+++ b/solution.py
@@ -69,8 +69,7 @@
     return first, -0.5 * first * first
 
 
-def image_of(coords, vis, first, second):
-    u, v, w = coords[0:1], coords[1:2], coords[2:3]
+def image_of(u, v, w, vis, first, second):
     linear = jnp.concatenate([u * first[:SUB], v * first[SUB:]], axis=0)
     cosine, sine = cos_sin_turns(linear + w * second)
     row_re, row_im = cosine[:SUB], sine[:SUB]
@@ -119,9 +118,29 @@
     )
 
 
-def screens_kernel(per_chunk, waits, own_ref, vis_ref, coords_ref, all_ref, image_ref, send_sems, ring_sems, pair_sems,
-                   own_sem):
-    tile = lax.axis_index("tile")
+def slot_row(tiles, rows, cols):
+    count, slots = tiles.shape[1], NT * CAP
+    slot = lax.broadcasted_iota(jnp.int32, (slots, count), 0)
+    named = tiles == (slot >> 1)
+    earlier = lax.broadcasted_iota(jnp.int32, (count, count), 0) < lax.broadcasted_iota(jnp.int32, (count, count), 1)
+    rank = jnp.dot(
+        named.astype(jnp.float32).astype(jnp.bfloat16), earlier.astype(jnp.float32).astype(jnp.bfloat16),
+        preferred_element_type=jnp.float32,
+    )
+    taken = named & (rank == (slot & 1).astype(jnp.float32))
+    value = (rows * TILE_SIDE + cols + 1).astype(jnp.float32)
+    column = jnp.sum(jnp.where(taken, value, 0.0), axis=1, keepdims=True)
+    shape = (slots, slots)
+    diagonal = lax.broadcasted_iota(jnp.int32, shape, 0) == lax.broadcasted_iota(jnp.int32, shape, 1)
+    line = jnp.sum(jnp.where(diagonal, jnp.broadcast_to(column, shape), 0.0), axis=0, keepdims=True)
+    return line.astype(jnp.int32) - 1
+
+
+def screens_kernel(per_chunk, waits, own_ref, vis_ref, coords_ref, tiles_ref, offsets_ref, all_ref, image_ref, table_ref,
+                   send_sems, ring_sems, pair_sems, own_sem, plane_out, plane_in, axis_out, axis_in):
+    corr, tile = lax.axis_index("corr"), lax.axis_index("tile")
+    planes, plane = lax.axis_size("corr"), lax.axis_size("tile")
+    me = corr * plane + tile
     core, y, z = tile % 2, tile // 2 % 4, tile // 8
 
     def chip(who, a, b):
@@ -132,12 +151,44 @@
     first_up, first_down = chip(core, 1, 0), chip(core, 3, 0)
     second_up, second_down = chip(core, 0, 1), chip(core, 0, 3)
     pair = (z * 4 + y) * 2 + (1 - core)
-    targets = (first_up, first_down, second_up, second_down, pair)
-
     barrier = pltpu.get_barrier_semaphore()
-    for target in targets:
-        pl.semaphore_signal(barrier, inc=1, device_id={"tile": target}, device_id_type=pl.DeviceIdType.MESH)
-    pl.semaphore_wait(barrier, len(targets))
+
+    def in_plane(t):
+        return {"tile": (tile + t) % plane}
+
+    def along(t):
+        return {"corr": (corr + t) % planes}
+
+    def greet(t, carry):
+        pl.semaphore_signal(barrier, inc=1, device_id=in_plane(t), device_id_type=pl.DeviceIdType.MESH)
+        return carry
+
+    lax.fori_loop(1, plane, greet, 0)
+    for t in range(1, planes):
+        pl.semaphore_signal(barrier, inc=1, device_id=along(t), device_id_type=pl.DeviceIdType.MESH)
+    table_ref[pl.ds(me, 1)] = slot_row(tiles_ref[...], offsets_ref[0:1], offsets_ref[1:2])[None]
+    pl.semaphore_wait(barrier, plane + planes - 2)
+
+    def plane_copy(t, source):
+        return pltpu.make_async_remote_copy(
+            src_ref=table_ref.at[source], dst_ref=table_ref.at[source], send_sem=plane_out.at[t], recv_sem=plane_in.at[t],
+            device_id=in_plane(t), device_id_type=pl.DeviceIdType.MESH,
+        )
+
+    def axis_copy(t, source):
+        rows = table_ref.at[pl.ds(source * plane, plane)]
+        return pltpu.make_async_remote_copy(
+            src_ref=rows, dst_ref=rows, send_sem=axis_out.at[t], recv_sem=axis_in.at[t],
+            device_id=along(t), device_id_type=pl.DeviceIdType.MESH,
+        )
+
+    def plane_start(t, carry):
+        plane_copy(t, me).start()
+        return carry
+
+    def plane_wait(t, carry):
+        plane_copy(t, corr * plane + (tile + plane - t) % plane).wait()
+        return carry
 
     half = own_ref.shape[0] // 2
     sent = []
@@ -206,7 +257,8 @@
 
     def compute(begin, end):
         def step(s, carry):
-            image_re, image_im = image_of(coords_ref[s], vis_ref[s], first, second)
+            u, v, w = (coords_ref[axis, pl.ds(s, 1)] for axis in range(3))
+            image_re, image_im = image_of(u, v, w, vis_ref[s], first, second)
             image_ref[s, 0:SUB] = image_re
             image_ref[s, SUB:2 * SUB] = image_im
             return carry
@@ -219,6 +271,17 @@
 
     def chunk(i, carry):
         compute(i * per_chunk, (i + 1) * per_chunk)
+
+        @pl.when(i == 0)
+        def _():
+            lax.fori_loop(1, plane, plane_start, 0)
+
+        @pl.when(i == chunks - 4)
+        def _():
+            lax.fori_loop(1, plane, plane_wait, 0)
+            for t in range(1, planes):
+                axis_copy(t, corr).start()
+
         for group, when in zip(groups, waits):
             if when is not None:
                 @pl.when(i == when)
@@ -240,13 +303,15 @@
                 await_pair((a, b, h))
     for number, unit in enumerate(sent):
         copy_of(unit, pair, pair_sems.at[0], number).wait_send()
+    for t in range(1, planes):
+        axis_copy(t, (corr + planes - t) % planes).wait()
     local.wait()
 
 
 WAITS = (3, 4, 5, 6, 7, 9, 11, 13, None, None, None, None)
 
 
-def gather_screens(own, visibilities, coords, tile_size):
+def gather_screens(own, visibilities, coords, tiles, offsets, devices, tile_size):
     count = visibilities.shape[0]
     vmem = pl.BlockSpec(memory_space=pltpu.VMEM)
     own_count = own.shape[0]
@@ -256,18 +321,23 @@
         out_shape=(
             jax.ShapeDtypeStruct((own_count * tile_size,) + own.shape[1:], own.dtype),
             jax.ShapeDtypeStruct((count, 2 * SUB, LANES), jnp.float32),
+            jax.ShapeDtypeStruct((devices, 1, NT * CAP), jnp.int32),
         ),
-        in_specs=[vmem, vmem, vmem],
-        out_specs=(pl.BlockSpec(memory_space=pl.ANY), vmem),
+        in_specs=[vmem] * 5,
+        out_specs=(pl.BlockSpec(memory_space=pl.ANY), vmem, vmem),
         scratch_shapes=[
             pltpu.SemaphoreType.DMA((copies,)),
             pltpu.SemaphoreType.DMA((32,)),
             pltpu.SemaphoreType.DMA((32,)),
             pltpu.SemaphoreType.DMA,
+            pltpu.SemaphoreType.DMA((tile_size,)),
+            pltpu.SemaphoreType.DMA((tile_size,)),
+            pltpu.SemaphoreType.DMA((devices // tile_size,)),
+            pltpu.SemaphoreType.DMA((devices // tile_size,)),
         ],
         compiler_params=pltpu.CompilerParams(vmem_limit_bytes=VMEM_LIMIT, collective_id=0, has_side_effects=True),
         name="screens",
-    )(own, visibilities, coords)
+    )(own, visibilities, coords, tiles, offsets)
 
 
 def sandwich_of(image, near, far):
@@ -329,10 +399,10 @@
     return [(-o[0], -o[1]) if k % 2 else o for k, o in enumerate(out)]
 
 
-def blocks_kernel(count, stations, tile_ids, offsets, image_ref, taper_ref, table_ref, screens, send_ref, meta_ref,
-                  near_far, x_re, x_im, y_ref, u_re, u_im, used, sems):
+def blocks_kernel(count, stations, tile_ids, image_ref, taper_ref, table_ref, screens, send_ref, near_far, x_re,
+                  x_im, y_ref, u_re, u_im, used, sems):
     def fetch(s, which):
-        return pltpu.make_async_copy(screens.at[stations[s, which]], near_far.at[s, which], sems.at[s, which])
+        return pltpu.make_async_copy(screens.at[stations[which, s]], near_far.at[s, which], sems.at[s, which])
 
     def start(s, carry):
         fetch(s, 0).start()
@@ -347,11 +417,6 @@
 
     lax.fori_loop(0, NT, clear, 0)
 
-    def clear_meta(i, carry):
-        meta_ref[i] = -1
-        return carry
-
-    lax.fori_loop(0, NT * CAP, clear_meta, 0)
     taper = taper_ref[...]
 
     def sandwich(s, carry):
@@ -392,7 +457,6 @@
         rank = used[tile]
         used[tile] = rank + 1
         slot = tile * CAP + rank
-        meta_ref[slot] = offsets[s, 0] * TILE_SIDE + offsets[s, 1]
         target = pl.ds(pl.multiple_of(slot * 2 * NJ, 2 * NJ), 2 * NJ)
         for e in range(NCORR):
             rows = pl.ds(pl.multiple_of(s * SUB + e * NJ, NJ), NJ)
@@ -402,7 +466,7 @@
     lax.fori_loop(0, count, pack, 0, unroll=2)
 
 
-def blocks(image, screens, stations, tile_ids, offsets):
+def blocks(image, screens, stations, tile_ids):
     count = image.shape[0]
     vmem = pl.BlockSpec(memory_space=pltpu.VMEM)
     smem = pl.BlockSpec(memory_space=pltpu.SMEM)
@@ -410,12 +474,9 @@
     points = count * NCORR
     return pl.pallas_call(
         functools.partial(blocks_kernel, count),
-        out_shape=(
-            jax.ShapeDtypeStruct((NCORR, slots * 2 * NJ, LANES), jnp.bfloat16),
-            jax.ShapeDtypeStruct((slots,), jnp.int32),
-        ),
-        in_specs=[smem, smem, smem, vmem, vmem, vmem, pl.BlockSpec(memory_space=pl.ANY)],
-        out_specs=(vmem, smem),
+        out_shape=jax.ShapeDtypeStruct((NCORR, slots * 2 * NJ, LANES), jnp.bfloat16),
+        in_specs=[smem, smem, vmem, vmem, vmem, pl.BlockSpec(memory_space=pl.ANY)],
+        out_specs=vmem,
         scratch_shapes=[
             pltpu.VMEM((count, 2, 2 * SUB, LANES), jnp.bfloat16),
             pltpu.VMEM((points * NJ, LANES), jnp.float32),
@@ -428,157 +489,129 @@
         ],
         compiler_params=pltpu.CompilerParams(vmem_limit_bytes=VMEM_LIMIT),
         name="blocks",
-    )(stations, tile_ids, offsets, image, taper_table(), uv_tables(), screens)
-
-
-def exchange_kernel(send_ref, meta_ref, recv_ref, table_ref, data_out, data_in, meta_out, meta_in, own_sem, stage):
+    )(stations, tile_ids, image, taper_table(), uv_tables(), screens)
+
+
+def exchange_kernel(per_owner, table, send_ref, out_ref, recv, moved, acc, data_out, data_in, own_sem):
     corr, tile = lax.axis_index("corr"), lax.axis_index("tile")
+    planes, plane = lax.axis_size("corr"), lax.axis_size("tile")
+    devices = planes * plane
     core, y, z = tile % 2, tile // 2 % 4, tile // 8
-    devices = recv_ref.shape[0]
-    me = corr * (devices // 4) + tile
+    slots = per_owner * CAP
 
     def there(k, sign):
-        x1 = (corr + sign * (k // 32 % 4) + 4) % 4
-        z1 = (z + sign * (k // 8 % 4) + 4) % 4
-        y1 = (y + sign * (k // 2 % 4) + 4) % 4
-        c1 = (core + k) % 2
-        return x1, (z1 * 4 + y1) * 2 + c1
-
-    def device(k):
-        x1, t1 = there(k, 1)
-        return {"corr": x1, "tile": t1}
+        d = k * ORDER % devices
+        x1 = (corr + sign * (d // 32 % 4) + 4) % 4
+        z1 = (z + sign * (d // 8 % 4) + 4) % 4
+        y1 = (y + sign * (d // 2 % 4) + 4) % 4
+        return x1, (z1 * 4 + y1) * 2 + (core + d) % 2
 
     barrier = pltpu.get_barrier_semaphore()
 
     def greet(k, carry):
-        pl.semaphore_signal(barrier, inc=1, device_id=device(k), device_id_type=pl.DeviceIdType.MESH)
+        x1, t1 = there(k, -1)
+        pl.semaphore_signal(barrier, inc=1, device_id={"corr": x1, "tile": t1}, device_id_type=pl.DeviceIdType.MESH)
         return carry
 
     lax.fori_loop(1, devices, greet, 0)
-    take = pltpu.make_async_copy(send_ref.at[me], stage, own_sem)
-    take.start()
-    take.wait()
-    put = pltpu.make_async_copy(stage, recv_ref.at[me], own_sem)
-    put.start()
-    put.wait()
-    put = pltpu.make_async_copy(meta_ref.at[0], table_ref.at[me], own_sem)
-    put.start()
-    put.wait()
+    own = pltpu.make_async_copy(send_ref.at[corr * plane + tile], recv.at[0], own_sem)
+    own.start()
+    acc[...] = jnp.zeros_like(acc)
     pl.semaphore_wait(barrier, devices - 1)
 
-    def data_copy(k):
+    def copy_of(k):
         x1, t1 = there(k, 1)
         return pltpu.make_async_remote_copy(
-            src_ref=send_ref.at[x1 * (devices // 4) + t1], dst_ref=recv_ref.at[me],
-            send_sem=data_out.at[k], recv_sem=data_in.at[k],
+            src_ref=send_ref.at[x1 * plane + t1], dst_ref=recv.at[k], send_sem=data_out.at[k], recv_sem=data_in.at[k],
             device_id={"corr": x1, "tile": t1}, device_id_type=pl.DeviceIdType.MESH,
         )
 
-    def meta_copy(k):
-        return pltpu.make_async_remote_copy(
-            src_ref=meta_ref.at[0], dst_ref=table_ref.at[me],
-            send_sem=meta_out.at[k], recv_sem=meta_in.at[k], device_id=device(k), device_id_type=pl.DeviceIdType.MESH,
-        )
-
     def start(k, carry):
-        meta_copy(k).start()
-        data_copy(k).start()
+        copy_of(k).start()
         return carry
 
     lax.fori_loop(1, devices, start, 0)
-
-    def finish(k, carry):
-        x1, t1 = there(k, -1)
-        source = x1 * (devices // 4) + t1
-        pltpu.make_async_remote_copy(
-            src_ref=send_ref.at[source], dst_ref=recv_ref.at[source], send_sem=data_out.at[k], recv_sem=data_in.at[k],
-            device_id={"corr": x1, "tile": t1}, device_id_type=pl.DeviceIdType.MESH,
-        ).wait()
-        pltpu.make_async_remote_copy(
-            src_ref=meta_ref.at[0], dst_ref=table_ref.at[source], send_sem=meta_out.at[k], recv_sem=meta_in.at[k],
-            device_id={"corr": x1, "tile": t1}, device_id_type=pl.DeviceIdType.MESH,
-        ).wait()
-        return carry
-
-    lax.fori_loop(1, devices, finish, 0)
-
-
-def exchange(sending, meta):
+    own.wait()
+
+    lane = lax.broadcasted_iota(jnp.int32, (NJ, LANES), 1)
+    batch = 4
+    depth = batch * CAP * SUB
+    target_lane = lax.broadcasted_iota(jnp.int32, (1, depth), 1)
+    target_row = lax.broadcasted_iota(jnp.int32, (TILE_SIDE, depth), 0)
+
+    def group(g, carry):
+        firsts = [jnp.zeros((1, depth), jnp.int32) for _ in range(per_owner)]
+        for i in range(batch):
+            k = g * batch + i
+
+            @pl.when(k > 0)
+            def _():
+                copy_of(k).wait()
+
+            x1, t1 = there(k, -1)
+            source = x1 * plane + t1
+            for slot in range(slots):
+                place = table[source, tile * slots + slot]
+                row0, col0 = place >> 7, place & (TILE_SIDE - 1)
+                begin = jnp.where(place >= 0, row0, 2 * LANES)
+                inside = (lane >= begin) & (lane < begin + SUB)
+                block = recv[k, slot * 2 * NJ:(slot + 1) * 2 * NJ].astype(jnp.float32)
+                number = i * CAP + slot % CAP
+                for part in range(2):
+                    data = block[part * NJ:(part + 1) * NJ]
+                    rolled = []
+                    for a4 in range(4):
+                        shift = (row0 + (LANES - a4 * SUB)) & (LANES - 1)
+                        rolled.append(jnp.where(inside, pltpu.roll(data, shift, 1), 0.0))
+                    rolled = jnp.concatenate(rolled, axis=0).astype(jnp.bfloat16)
+                    moved[slot // CAP, number * SUB:(number + 1) * SUB, part * LANES:(part + 1) * LANES] = rolled
+                firsts[slot // CAP] = jnp.where(target_lane >= number * SUB, col0 - number * SUB, firsts[slot // CAP])
+        for own_tile in range(per_owner):
+            select = (target_row == firsts[own_tile] + target_lane).astype(jnp.float32).astype(jnp.bfloat16)
+            acc[own_tile] += jnp.dot(select, moved[own_tile], preferred_element_type=jnp.float32)
+        return carry
+
+    lax.fori_loop(0, devices // batch, group, 0)
+    for own_tile in range(per_owner):
+        for part in range(2):
+            out_ref[own_tile, part] = acc[own_tile, :, part * LANES:(part + 1) * LANES].T
+
+
+ORDER = 37
+
+
+def exchange(sending, table, per_owner):
     devices = sending.shape[0]
-    hbm = pl.BlockSpec(memory_space=pl.ANY)
-    vmem = pl.BlockSpec(memory_space=pltpu.VMEM)
     sems = pltpu.SemaphoreType.DMA((devices,))
     return pl.pallas_call(
-        exchange_kernel,
-        out_shape=(
-            jax.ShapeDtypeStruct(sending.shape, sending.dtype),
-            jax.ShapeDtypeStruct((devices,) + meta.shape[1:], meta.dtype),
-        ),
-        in_specs=[hbm, vmem],
-        out_specs=(hbm, vmem),
-        scratch_shapes=[sems, sems, sems, sems, pltpu.SemaphoreType.DMA, pltpu.VMEM(sending.shape[1:], sending.dtype)],
+        functools.partial(exchange_kernel, per_owner),
+        out_shape=jax.ShapeDtypeStruct((per_owner, 2, TILE_SIDE, TILE_SIDE), jnp.float32),
+        in_specs=[pl.BlockSpec(memory_space=pltpu.SMEM), pl.BlockSpec(memory_space=pl.ANY)],
+        out_specs=pl.BlockSpec(memory_space=pltpu.VMEM),
+        scratch_shapes=[
+            pltpu.VMEM(sending.shape, sending.dtype),
+            pltpu.VMEM((per_owner, 4 * CAP * SUB, 2 * LANES), jnp.bfloat16),
+            pltpu.VMEM((per_owner, TILE_SIDE, 2 * LANES), jnp.float32),
+            sems,
+            sems,
+            pltpu.SemaphoreType.DMA,
+        ],
         compiler_params=pltpu.CompilerParams(vmem_limit_bytes=VMEM_LIMIT, collective_id=1, has_side_effects=True),
         name="exchange",
-    )(sending, meta)
-
-
-def gather_kernel(sources, per_owner, table, recv_ref, out_ref, acc):
-    acc[...] = jnp.zeros_like(acc)
-    lane = lax.broadcasted_iota(jnp.int32, (NJ, LANES), 1)
-    slots = per_owner * CAP
-    own = lax.axis_index("tile") * slots
-
-    def step(src, carry):
-        for slot in range(slots):
-            place = table[src, own + slot]
-            valid = place >= 0
-            row0 = jnp.where(valid, place >> 7, 0)
-            col0 = jnp.where(valid, place & (TILE_SIDE - 1), 0)
-            begin = jnp.where(valid, row0, 2 * LANES)
-            inside = (lane >= begin) & (lane < begin + SUB)
-            block = recv_ref[src, slot * 2 * NJ:(slot + 1) * 2 * NJ].astype(jnp.float32)
-            for part in range(2):
-                data = block[part * NJ:(part + 1) * NJ]
-                moved = []
-                for a4 in range(4):
-                    shift = (row0 + (LANES - a4 * SUB)) & (LANES - 1)
-                    moved.append(jnp.where(inside, pltpu.roll(data, shift, 1), 0.0))
-                rows = pl.ds(col0, SUB)
-                acc[slot, part, rows] = acc[slot, part, rows] + jnp.concatenate(moved, axis=0)
-        return carry
-
-    lax.fori_loop(0, sources, step, 0, unroll=2)
-    for tile in range(per_owner):
-        for part in range(2):
-            total = acc[tile * CAP, part]
-            for rank in range(1, CAP):
-                total = total + acc[tile * CAP + rank, part]
-            out_ref[tile, part] = total.T
-
-
-def gather_blocks(received, meta, per_owner):
-    sources = received.shape[0]
-    vmem = pl.BlockSpec(memory_space=pltpu.VMEM)
-    return pl.pallas_call(
-        functools.partial(gather_kernel, sources, per_owner),
-        out_shape=jax.ShapeDtypeStruct((per_owner, 2, TILE_SIDE, TILE_SIDE), jnp.float32),
-        in_specs=[pl.BlockSpec(memory_space=pltpu.SMEM), vmem],
-        out_specs=vmem,
-        scratch_shapes=[pltpu.VMEM((per_owner * CAP, 2, TILE_SIDE, TILE_SIDE), jnp.float32)],
-        compiler_params=pltpu.CompilerParams(vmem_limit_bytes=VMEM_LIMIT),
-        name="accumulate",
-    )(meta, received)
+    )(table, sending)
 
 
 def per_device(visibilities, coords, stations, tile_ids, offsets, screens):
     tile_size = lax.axis_size("tile")
+    devices = lax.axis_size("corr") * tile_size
     per_owner = NT // tile_size
     own = screens.reshape(screens.shape[0], 2 * SUB, LANES)
-    all_screens, image = gather_screens(own, visibilities, coords, tile_size)
-    sending, meta = blocks(image, all_screens, stations, tile_ids[:, 0], offsets)
-    rows = per_owner * CAP * 2 * NJ
-    received, table = exchange(sending.reshape(NCORR * tile_size, rows, LANES), meta.reshape(1, 1, NT * CAP))
-    return gather_blocks(received, table.reshape(-1, NT * CAP), per_owner)[None]
+    all_screens, image, table = gather_screens(
+        own, visibilities, coords.transpose(1, 0, 2), tile_ids.T, offsets.T, devices, tile_size
+    )
+    sending = blocks(image, all_screens, stations.T, tile_ids[:, 0])
+    sending = sending.reshape(devices, per_owner * CAP * 2 * NJ, LANES)
+    return exchange(sending, table.reshape(devices, NT * CAP), per_owner)[None]
 
 
 def solution(mesh):

time: 115 us -> 99.4 us (0.86)
  Pallas kernels: 108 us -> 95.5 us
  local copies, waits for them, and re-layouts: 6.31 us -> 3.44 us
    pallas_call x3 -> x2, Pallas kernels: 68.6 us -> 52.5 us  [the longest x1 43.9 us: exchange(): pl.pallas_call(functools.partial(exchange_kernel, per_owner), out_shape=j...]
    pallas_call x1, Pallas kernels: 39.3 us -> 43.1 us  [gather_screens(): pl.pallas_call(functools.partial(screens_kernel, 4, WAITS), out_shape=(ja...]
    unnamed x3 -> x1, local copies, waits for them, and re-layouts: 4.55 us -> 1.67 us
where the time goes in v2:
time: 99.4 us; the launch traced here: 99 us
  Pallas kernels  95.5 us (96%)
  local copies, waits for them, and re-layouts  3.44 us (3%)
    pallas_call x1, Pallas kernels, exchange(): pl.pallas_call(functools.partial(exchange_kernel, per_owner), out_shape=j...  43.9 us
    pallas_call x1, Pallas kernels, gather_screens(): pl.pallas_call(functools.partial(screens_kernel, 4, WAITS), out_shape=(ja...  43.1 us
    pallas_call x1, Pallas kernels, blocks(): pl.pallas_call(functools.partial(blocks_kernel, count), out_shape=jax.Sha...  8.61 us

profile of v2, /device:TPU:1, one launch (start us, length us, event | category | flops | bytes accessed | tf_op | source)
XLA Modules:
  0.0 99.0 jit_solution(8946879399921129704)
XLA Ops:
  0.0 1.8 %reshape.9.own_ref = bf16[16,64,128]{2,1,0:T(8,128)(2,1)} reshape(bf16[16,8,1024]{2,1,0:T(8,128)(2,1)} %param.13) | data formatting | bytes 524288 | tf_op jit(solution)/shard_map/reshape | solution.py:608
  1.8 43.1 %screens.1 = (bf16[512,64,128]{2,1,0:T(8,128)(2,1)}, f32[64,64,128]{2,1,0:T(8,128)}, s32[128,1,128]{2,1,0:T(1,128)}) custom-call(bf16[16,64,128]{2,1,0:T(8,128)(2,1)} %reshape.9.own_ref, bf16[64,8,256]{2,1,0:T(8,128)(2,1)} %vis_ref.1, f32[3,64,256]{2,1,0:T(8,128)} %bitcast.10, s32[1,64]{1,0:T(1,128)} %bitcast.12, s32[2,64]{1,0:T(2,128)} %bitcast.14), custom_call_target="tpu_custom_call" | custom-call | tf_op jit(solution)/shard_map/screens/pallas_call | solution.py:319
  44.8 8.6 %blocks.1 = bf16[4,2048,128]{2,1,0:T(8,128)(2,1)} custom-call(s32[2,64]{1,0:T(2,128)} %bitcast.15, s32[64]{0:T(128)} %bitcast.13, f32[64,64,128]{2,1,0:T(8,128)} %get-tuple-element.9.image_ref, f32[8,128]{1,0:T(8,128)} %constant.4.clone.taper_ref, bf16[8,256,256]{2,1,0:T(8,128)(2,1)} %constant.5.clone.table_ref, bf16[512,64,128]{2,1,0:T(8,128)(2,1)} %get-tuple-element.10.screens), custom_call_target="tpu_custom_call" | custom-call | tf_op jit(solution)/shard_map/blocks/pallas_call | solution.py:475
  53.4 43.9 %exchange.1 = f32[2,2,128,128]{3,2,1,0:T(8,128)} custom-call(s32[128,128]{1,0:T(8,128)} %bitcast.11, bf16[128,64,128]{2,1,0:T(8,128)(2,1)} %bitcast.8), custom_call_target="tpu_custom_call" | custom-call | tf_op jit(solution)/shard_map/exchange/pallas_call | solution.py:586
  97.3 1.7 %copy.10 = f32[1,2,2,128,128]{4,3,2,1,0:T(8,128)} copy(f32[1,2,2,128,128]{4,3,2,1,0:T(8,128)} %bitcast.9) | data formatting | bytes 524288

commit v3 on v2

--- a/solution.py
+++ b/solution.py
@@ -141,11 +141,11 @@
     corr, tile = lax.axis_index("corr"), lax.axis_index("tile")
     planes, plane = lax.axis_size("corr"), lax.axis_size("tile")
     me = corr * plane + tile
-    core, y, z = tile % 2, tile // 2 % 4, tile // 8
+    core, y, z = tile & 1, (tile >> 1) & 3, tile >> 3
 
     def chip(who, a, b):
-        there_z = (z + who * a + (1 - who) * b) % 4
-        there_y = (y + (1 - who) * a + who * b) % 4
+        there_z = (z + who * a + (1 - who) * b) & 3
+        there_y = (y + (1 - who) * a + who * b) & 3
         return (there_z * 4 + there_y) * 2 + who
 
     first_up, first_down = chip(core, 1, 0), chip(core, 3, 0)
@@ -154,10 +154,10 @@
     barrier = pltpu.get_barrier_semaphore()
 
     def in_plane(t):
-        return {"tile": (tile + t) % plane}
+        return {"tile": (tile + t) & (plane - 1)}
 
     def along(t):
-        return {"corr": (corr + t) % planes}
+        return {"corr": (corr + t) & (planes - 1)}
 
     def greet(t, carry):
         pl.semaphore_signal(barrier, inc=1, device_id=in_plane(t), device_id_type=pl.DeviceIdType.MESH)
@@ -187,7 +187,7 @@
         return carry
 
     def plane_wait(t, carry):
-        plane_copy(t, corr * plane + (tile + plane - t) % plane).wait()
+        plane_copy(t, corr * plane + ((tile - t) & (plane - 1))).wait()
         return carry
 
     half = own_ref.shape[0] // 2
@@ -304,7 +304,7 @@
     for number, unit in enumerate(sent):
         copy_of(unit, pair, pair_sems.at[0], number).wait_send()
     for t in range(1, planes):
-        axis_copy(t, (corr + planes - t) % planes).wait()
+        axis_copy(t, (corr - t) & (planes - 1)).wait()
     local.wait()
 
 
@@ -496,15 +496,15 @@
     corr, tile = lax.axis_index("corr"), lax.axis_index("tile")
     planes, plane = lax.axis_size("corr"), lax.axis_size("tile")
     devices = planes * plane
-    core, y, z = tile % 2, tile // 2 % 4, tile // 8
+    core, y, z = tile & 1, (tile >> 1) & 3, tile >> 3
     slots = per_owner * CAP
 
     def there(k, sign):
-        d = k * ORDER % devices
-        x1 = (corr + sign * (d // 32 % 4) + 4) % 4
-        z1 = (z + sign * (d // 8 % 4) + 4) % 4
-        y1 = (y + sign * (d // 2 % 4) + 4) % 4
-        return x1, (z1 * 4 + y1) * 2 + (core + d) % 2
+        d = (k * ORDER) & (devices - 1)
+        x1 = (corr + sign * (d >> 5)) & 3
+        z1 = (z + sign * (d >> 3)) & 3
+        y1 = (y + sign * (d >> 1)) & 3
+        return x1, z1 * 8 + y1 * 2 + ((core + d) & 1)
 
     barrier = pltpu.get_barrier_semaphore()
 

time: 99.4 us -> 102 us (1.026)
  the two profiles are of different devices: /device:TPU:1 before, /device:TPU:5 now
where the time goes in v3:
time: 102 us
  Pallas kernels  98.7 us (97%)
  local copies, waits for them, and re-layouts  3.44 us (3%)
    pallas_call x1, Pallas kernels, exchange(): pl.pallas_call(functools.partial(exchange_kernel, per_owner), out_shape=j...  48 us
    pallas_call x1, Pallas kernels, gather_screens(): pl.pallas_call(functools.partial(screens_kernel, 4, WAITS), out_shape=(ja...  42 us
    pallas_call x1, Pallas kernels, blocks(): pl.pallas_call(functools.partial(blocks_kernel, count), out_shape=jax.Sha...  8.61 us

profile of v3, /device:TPU:5, one launch (start us, length us, event | category | flops | bytes accessed | tf_op | source)
XLA Modules:
  0.0 102.1 jit_solution(319311512597442309)
XLA Ops:
  0.0 1.8 %reshape.9.own_ref = bf16[16,64,128]{2,1,0:T(8,128)(2,1)} reshape(bf16[16,8,1024]{2,1,0:T(8,128)(2,1)} %param.13) | data formatting | bytes 524288 | tf_op jit(solution)/shard_map/reshape | solution.py:608
  1.8 42.0 %screens.1 = (bf16[512,64,128]{2,1,0:T(8,128)(2,1)}, f32[64,64,128]{2,1,0:T(8,128)}, s32[128,1,128]{2,1,0:T(1,128)}) custom-call(bf16[16,64,128]{2,1,0:T(8,128)(2,1)} %reshape.9.own_ref, bf16[64,8,256]{2,1,0:T(8,128)(2,1)} %vis_ref.1, f32[3,64,256]{2,1,0:T(8,128)} %bitcast.10, s32[1,64]{1,0:T(1,128)} %bitcast.12, s32[2,64]{1,0:T(2,128)} %bitcast.14), custom_call_target="tpu_custom_call" | custom-call | tf_op jit(solution)/shard_map/screens/pallas_call | solution.py:319
  43.8 8.6 %blocks.1 = bf16[4,2048,128]{2,1,0:T(8,128)(2,1)} custom-call(s32[2,64]{1,0:T(2,128)} %bitcast.15, s32[64]{0:T(128)} %bitcast.13, f32[64,64,128]{2,1,0:T(8,128)} %get-tuple-element.9.image_ref, f32[8,128]{1,0:T(8,128)} %constant.4.clone.taper_ref, bf16[8,256,256]{2,1,0:T(8,128)(2,1)} %constant.5.clone.table_ref, bf16[512,64,128]{2,1,0:T(8,128)(2,1)} %get-tuple-element.10.screens), custom_call_target="tpu_custom_call" | custom-call | tf_op jit(solution)/shard_map/blocks/pallas_call | solution.py:475
  52.4 48.0 %exchange.1 = f32[2,2,128,128]{3,2,1,0:T(8,128)} custom-call(s32[128,128]{1,0:T(8,128)} %bitcast.11, bf16[128,64,128]{2,1,0:T(8,128)(2,1)} %bitcast.8), custom_call_target="tpu_custom_call" | custom-call | tf_op jit(solution)/shard_map/exchange/pallas_call | solution.py:586
  100.5 1.7 %copy.10 = f32[1,2,2,128,128]{4,3,2,1,0:T(8,128)} copy(f32[1,2,2,128,128]{4,3,2,1,0:T(8,128)} %bitcast.9) | data formatting | bytes 524288

commit v4 on v0

v4 whole, which is shorter than its diff:
```python
import functools
import math

import jax
import jax.numpy as jnp
import numpy as np
from jax import lax
from jax.experimental import pallas as pl
from jax.experimental.pallas import tpu as pltpu
from jax.sharding import PartitionSpec as P

SUB = 32
NT = 64
TILE_SIDE = 128
NVIS = 256
PIX = 1024
NCORR = 4
CAP = 2
NJ = 8
LANES = 128
SIN_POLY = (3.141592579805584, -5.167706866167941, 2.550031193519298, -0.5980441939119835, 0.07721838615698538)
COS_POLY = (0.9999999532476082, -4.934792830619647, 4.058411352862557, -1.3318765680805114, 0.2196896110968953)
ROOT_HALF = math.sqrt(0.5)
VMEM_LIMIT = 60 * 1024 * 1024


def uv_tables():
    rr = np.arange(4)[:, None, None, None]
    c = np.arange(SUB)[None, :, None, None]
    a4 = np.arange(4)[None, None, :, None]
    d = np.arange(SUB)[None, None, None, :]
    half = SUB // 2
    tables = []
    for a8 in range(NJ):
        turns = (rr * (a8 + 8 * a4 - half) + (c - half) * (d - half)) % SUB
        angle = (-2.0 * np.pi / SUB) * turns.reshape(LANES, LANES)
        re, im = np.cos(angle) / SUB, np.sin(angle) / SUB
        tables.append(np.block([[re, im], [-im, re]]))
    return jnp.asarray(np.stack(tables), jnp.bfloat16)


def taper_table():
    pos = (np.arange(SUB) - SUB // 2 + 0.5) / (SUB // 2)
    edge = 1.0 - 0.8 * pos * pos
    return jnp.asarray((edge[:, None] * edge[None, :] / NVIS).reshape(NJ, LANES), jnp.float32)


def poly(square, coefficients):
    total = jnp.full_like(square, coefficients[-1])
    for coefficient in coefficients[-2::-1]:
        total = total * square + coefficient
    return total


def cos_sin_turns(turns):
    rest = turns - jnp.round(turns)
    square = rest * rest
    sine = rest * poly(square, SIN_POLY)
    cosine = poly(square, COS_POLY)
    twice = sine + sine
    return 1.0 - twice * sine, twice * cosine


def direction_tables():
    row = lax.broadcasted_iota(jnp.int32, (2 * SUB, NVIS), 0)
    r = (row % NJ) * 4 + row // NJ
    place = jnp.where(row < SUB, r, row - SUB)
    first = (place - SUB // 2).astype(jnp.float32) * (1.0 / SUB)
    return first, -0.5 * first * first


def image_of(u, v, w, vis, first, second):
    linear = jnp.concatenate([u * first[:SUB], v * first[SUB:]], axis=0)
    cosine, sine = cos_sin_turns(linear + w * second)
    row_re, row_im = cosine[:SUB], sine[:SUB]
    col_re, col_im = cosine[SUB:], sine[SUB:]
    vis = vis.astype(jnp.float32)
    lhs = []
    for rr in range(4):
        a_re, a_im = row_re[rr * NJ:(rr + 1) * NJ], row_im[rr * NJ:(rr + 1) * NJ]
        part_re, part_im = [], []
        for e in range(NCORR):
            v_re, v_im = vis[e:e + 1], vis[NCORR + e:NCORR + e + 1]
            part_re.append(v_re * a_re - v_im * a_im)
            part_im.append(v_re * a_im + v_im * a_re)
        lhs.append(jnp.concatenate([jnp.concatenate(part_re, axis=0), jnp.concatenate(part_im, axis=0)], axis=1))
    lhs = jnp.concatenate(lhs, axis=0).astype(jnp.bfloat16)
    upper = jnp.concatenate([col_re, -col_im], axis=1)
    lower = jnp.concatenate([col_im, col_re], axis=1)
    rhs = jnp.concatenate([upper, lower, upper, lower], axis=0).astype(jnp.bfloat16)
    out = lax.dot_general(lhs, rhs, (((1,), (1,)), ((), ())), preferred_element_type=jnp.float32)
    parts = [out[rr * SUB:(rr + 1) * SUB] for rr in range(4)]
    turned = [pltpu.roll(part, SUB, 1) for part in parts]
    lane = lax.broadcasted_iota(jnp.int32, (SUB, LANES), 1)

    def join(a, b, c, d):
        return jnp.where(lane < SUB, a, jnp.where(lane < 2 * SUB, b, jnp.where(lane < 3 * SUB, c, d)))

    image_re = join(parts[0], turned[1], parts[2], turned[3])
    image_im = join(turned[0], parts[1], turned[2], parts[3])
    return image_re, image_im


def ring_plan():
    return (
        ((3, 0, 0), (1, 0, 1)),
        ((3, 0, 1), (1, 0, 0)),
        ((0, 3, 0), (0, 1, 1)),
        ((0, 3, 1), (0, 1, 0)),
        ((2, 0, 0), (2, 0, 1)),
        ((3, 3, 0), (3, 1, 1), (1, 3, 0), (1, 1, 1)),
        ((0, 2, 0), (0, 2, 1)),
        ((3, 3, 1), (3, 1, 0), (1, 3, 1), (1, 1, 0)),
        ((2, 3, 0), (2, 1, 1)),
        ((3, 2, 0), (3, 2, 1), (1, 2, 0), (1, 2, 1)),
        ((2, 3, 1), (2, 1, 0)),
        ((2, 2, 0), (2, 2, 1)),
    )


def sandwich_of(image, near, far):
    def row(array, index):
        return array[index * NJ:(index + 1) * NJ]

    mid_re, mid_im = {}, {}
    for out_row in range(2):
        for inner in range(2):
            total_re = total_im = None
            for first in range(2):
                n_re, n_im = row(near, 2 * first + out_row), row(near, 4 + 2 * first + out_row)
                v_re, v_im = row(image, 2 * first + inner), row(image, 4 + 2 * first + inner)
                re = n_re * v_re + n_im * v_im
                im = n_re * v_im - n_im * v_re
                total_re = re if total_re is None else total_re + re
                total_im = im if total_im is None else total_im + im
            mid_re[out_row, inner], mid_im[out_row, inner] = total_re, total_im
    out_re, out_im = [], []
    for out_row in range(2):
        for out_col in range(2):
            total_re = total_im = None
            for inner in range(2):
                m_re, m_im = mid_re[out_row, inner], mid_im[out_row, inner]
                f_re, f_im = row(far, 2 * inner + out_col), row(far, 4 + 2 * inner + out_col)
                re = m_re * f_re - m_im * f_im
                im = m_re * f_im + m_im * f_re
                total_re = re if total_re is None else total_re + re
                total_im = im if total_im is None else total_im + im
            out_re.append(total_re)
            out_im.append(total_im)
    return out_re, out_im


def fft8(re, im):
    def add(x, y):
        return x[0] + y[0], x[1] + y[1]

    def sub(x, y):
        return x[0] - y[0], x[1] - y[1]

    def turn(x):
        return x[1], -x[0]

    def fft4(x):
        even_add, even_sub = add(x[0], x[2]), sub(x[0], x[2])
        odd_add, odd_sub = add(x[1], x[3]), turn(sub(x[1], x[3]))
        return [add(even_add, odd_add), add(even_sub, odd_sub), sub(even_add, odd_add), sub(even_sub, odd_sub)]

    x = list(zip(re, im))
    even, odd = fft4(x[0::2]), fft4(x[1::2])
    odd = [
        odd[0],
        ((odd[1][0] + odd[1][1]) * ROOT_HALF, (odd[1][1] - odd[1][0]) * ROOT_HALF),
        turn(odd[2]),
        ((odd[3][1] - odd[3][0]) * ROOT_HALF, (-odd[3][0] - odd[3][1]) * ROOT_HALF),
    ]
    out = [add(even[k], odd[k]) for k in range(4)] + [sub(even[k], odd[k]) for k in range(4)]
    return [(-o[0], -o[1]) if k % 2 else o for k, o in enumerate(out)]


def one_hot(mask):
    return mask.astype(jnp.float32).astype(jnp.bfloat16)


def diagonal(n):
    return lax.broadcasted_iota(jnp.int32, (n, n), 0) == lax.broadcasted_iota(jnp.int32, (n, n), 1)


def as_line(column):
    n = column.shape[0]
    return jnp.sum(jnp.where(diagonal(n), jnp.broadcast_to(column, (n, n)), 0), axis=0, keepdims=True)


def slot_lines(tiles, rows, cols):
    count, slots = tiles.shape[1], NT * CAP
    shape = (count, count)
    wide = jnp.broadcast_to(tiles, shape)
    column = jnp.sum(jnp.where(diagonal(count), wide, 0), axis=1, keepdims=True)
    earlier = lax.broadcasted_iota(jnp.int32, shape, 0) < lax.broadcasted_iota(jnp.int32, shape, 1)
    rank = jnp.sum(jnp.where(earlier & (column == wide), 1, 0), axis=0, keepdims=True)
    slot = lax.broadcasted_iota(jnp.int32, (slots, count), 0)
    taken = tiles * CAP + rank == slot
    number = lax.broadcasted_iota(jnp.int32, (slots, count), 1)

    def total(values):
        return as_line(jnp.sum(jnp.where(taken, values, 0), axis=1, keepdims=True))

    return total(number), total(rows + 1) - 1, total(cols)


def grid_kernel(per_chunk, waits, per_owner, stations, own_ref, vis_ref, coords_ref, tiles_ref, offsets_ref, taper_ref,
                uv_ref, out_ref, shards, meta, image, x_re, x_im, y_ref, u_re, u_im, send, recv, moved, acc, order_row,
                order, places_row, places, send_sems, ring_sems, pair_sems, axis_out, axis_in, data_out, data_in, own_sem):
    corr, tile = lax.axis_index("corr"), lax.axis_index("tile")
    planes, plane = lax.axis_size("corr"), lax.axis_size("tile")
    devices = planes * plane
    core, y, z = tile & 1, (tile >> 1) & 3, tile >> 3
    count = vis_ref.shape[0]
    owned = own_ref.shape[0]
    groups_owned = shards.shape[1] - 1
    half = groups_owned // 2

    def chip(who, a, b):
        there_z = (z + who * a + (1 - who) * b) & 3
        there_y = (y + (1 - who) * a + who * b) & 3
        return (there_z * 4 + there_y) * 2 + who

    first_up, first_down = chip(core, 1, 0), chip(core, 3, 0)
    second_up, second_down = chip(core, 0, 1), chip(core, 0, 3)
    pair = (z * 4 + y) * 2 + (1 - core)
    targets = (first_up, first_down, second_up, second_down, pair)

    def along(t):
        return {"corr": (corr + t) & (planes - 1)}

    barrier = pltpu.get_barrier_semaphore()
    for target in targets:
        pl.semaphore_signal(barrier, inc=1, device_id={"tile": target}, device_id_type=pl.DeviceIdType.MESH)
    for t in range(1, planes):
        pl.semaphore_signal(barrier, inc=1, device_id=along(t), device_id_type=pl.DeviceIdType.MESH)

    for i in range(owned):
        screen = own_ref[i].astype(jnp.float32)
        for j in range(NJ):
            x_re[pl.ds(i * 2 * SUB + j, NJ, stride=NJ)] = screen[:, j * LANES:(j + 1) * LANES]
    for i in range(owned):
        screen = x_re[i * 2 * SUB:(i + 1) * 2 * SUB].astype(jnp.bfloat16)
        shards[tile, i * PARTS:(i + 1) * PARTS] = screen.reshape(PARTS, META, LANES)
    number_line, row_line, col_line = slot_lines(tiles_ref[...], offsets_ref[0:1], offsets_ref[1:2])
    kind = lax.broadcasted_iota(jnp.int32, (META, LANES), 0)
    lines = jnp.where(kind == 0, row_line, jnp.where(kind == 1, col_line, 0))
    shards[tile, groups_owned] = lines.astype(jnp.float32).astype(jnp.bfloat16)
    order_row[...] = number_line
    pl.semaphore_wait(barrier, len(targets) + planes - 1)

    sent = []

    def place(owner, h):
        return shards.at[owner, pl.ds(h * half, half + h)]

    def unit_index(unit):
        return (unit[0] * 4 + unit[1]) * 2 + unit[2]

    def unit_copy(owner, h, target, send_sem, sem):
        return pltpu.make_async_remote_copy(
            src_ref=place(owner, h), dst_ref=place(owner, h), send_sem=send_sem, recv_sem=sem,
            device_id={"tile": target}, device_id_type=pl.DeviceIdType.MESH,
        )

    def push(unit, target, arrives):
        sem = pair_sems.at[unit_index(unit)] if arrives is None else ring_sems.at[unit_index(arrives)]
        unit_copy(chip(core, unit[0], unit[1]), unit[2], target, send_sems.at[len(sent)], sem).start()
        sent.append(unit)

    def await_ring(unit):
        owner = chip(core, unit[0], unit[1])
        unit_copy(owner, unit[2], pair, send_sems.at[0], ring_sems.at[unit_index(unit)]).wait_recv()

    def await_pair(unit):
        owner = chip(1 - core, unit[0], unit[1])
        unit_copy(owner, unit[2], pair, send_sems.at[0], pair_sems.at[unit_index(unit)]).wait_recv()

    def forward(unit):
        a, b, h = unit
        if b == 0:
            if (a, h) == (3, 0):
                push(unit, first_up, (2, 0, 0))
            if (a, h) == (1, 1):
                push(unit, first_down, (2, 0, 1))
            up, down = (second_up, (a, 3, h)), (second_down, (a, 1, h))
            for target, arrives in (up, down) if h == 0 else (down, up):
                push(unit, target, arrives)
        elif (b, h) == (3, 0):
            push(unit, second_up, (a, 2, 0))
        elif (b, h) == (1, 1):
            push(unit, second_down, (a, 2, 1))
        push(unit, pair, None)

    push((0, 0, 0), first_up, (3, 0, 0))
    push((0, 0, 1), first_down, (1, 0, 1))
    push((0, 0, 1), first_up, (3, 0, 1))
    push((0, 0, 0), first_down, (1, 0, 0))
    push((0, 0, 0), second_up, (0, 3, 0))
    push((0, 0, 1), second_down, (0, 1, 1))
    push((0, 0, 1), second_up, (0, 3, 1))
    push((0, 0, 0), second_down, (0, 1, 0))
    for h in range(2):
        push((0, 0, h), pair, None)

    first, second = direction_tables()

    def compute(begin, end):
        def step(s, carry):
            u, v, w = (coords_ref[axis, pl.ds(s, 1)] for axis in range(3))
            image_re, image_im = image_of(u, v, w, vis_ref[s], first, second)
            image[s, 0:SUB] = image_re
            image[s, SUB:2 * SUB] = image_im
            return carry

        lax.fori_loop(begin, end, step, 0)

    groups = ring_plan()
    chunks = count // per_chunk

    def chunk(i, carry):
        compute(i * per_chunk, (i + 1) * per_chunk)
        for group, when in zip(groups, waits):
            if when is not None:
                @pl.when(i == when)
                def _():
                    for unit in group:
                        await_ring(unit)
                        forward(unit)
        return carry

    lax.fori_loop(0, chunks, chunk, 0)
    scalars = pltpu.make_async_copy(order_row, order, own_sem)
    scalars.start()
    for group, when in zip(groups, waits):
        if when is None:
            for unit in group:
                await_ring(unit)
                forward(unit)
    for a in range(4):
        for b in range(4):
            for h in range(2):
                await_pair((a, b, h))

    def axis_copy(t, whose):
        return pltpu.make_async_remote_copy(
            src_ref=shards.at[:, groups_owned], dst_ref=meta.at[whose],
            send_sem=axis_out.at[t], recv_sem=axis_in.at[t], device_id=along(t), device_id_type=pl.DeviceIdType.MESH,
        )

    for t in range(1, planes):
        axis_copy(t, corr).start()
    meta[corr] = shards[:, groups_owned]

    taper = taper_ref[...]

    def screen_of(station):
        screen = shards[station >> 4, pl.ds((station & (owned - 1)) * PARTS, PARTS)]
        return screen.reshape(2 * SUB, LANES).astype(jnp.float32)

    def sandwich(s, carry):
        out_re, out_im = sandwich_of(image[s], screen_of(stations[0, s]), screen_of(stations[1, s]))
        for e in range(NCORR):
            rows = pl.ds(pl.multiple_of(s * SUB + e * NJ, NJ), NJ)
            x_re[rows] = out_re[e] * taper
            x_im[rows] = out_im[e] * taper
        return carry

    lax.fori_loop(0, count, sandwich, 0, unroll=2)
    points = 16

    def transform(i, carry):
        base = i * (points * NJ)
        re = [x_re[pl.ds(base + j, points, stride=NJ)] for j in range(NJ)]
        im = [x_im[pl.ds(base + j, points, stride=NJ)] for j in range(NJ)]
        rows = pl.ds(pl.multiple_of(i * points, points), points)
        for a8, (y_re, y_im) in enumerate(fft8(re, im)):
            y_ref[a8, rows, 0:LANES] = y_re.astype(jnp.bfloat16)
            y_ref[a8, rows, LANES:2 * LANES] = y_im.astype(jnp.bfloat16)
        return carry

    lax.fori_loop(0, count * NCORR // points, transform, 0)
    for a8 in range(NJ):
        out = jnp.dot(y_ref[a8], uv_ref[a8], preferred_element_type=jnp.float32)
        u_re[pl.ds(a8, count * NCORR, stride=NJ)] = out[:, 0:LANES]
        u_im[pl.ds(a8, count * NCORR, stride=NJ)] = out[:, LANES:2 * LANES]

    slots = per_owner * CAP
    scalars.wait()

    def pack(owner, carry):
        for slot in range(slots):
            s = order[0, owner * slots + slot]
            for e in range(NCORR):
                rows = pl.ds(s * SUB + e * NJ, NJ)
                both = jnp.concatenate([u_re[rows], u_im[rows]], axis=0)
                send[e * plane + owner, slot * 2 * NJ:(slot + 1) * 2 * NJ] = both.astype(jnp.bfloat16)
        return carry

    lax.fori_loop(0, plane, pack, 0)
    for t in range(1, planes):
        axis_copy(t, (corr - t) & (planes - 1)).wait()

    def there(k, sign):
        d = (k * ORDER) & (devices - 1)
        x1 = (corr + sign * (d >> 5)) & 3
        z1 = (z + sign * (d >> 3)) & 3
        y1 = (y + sign * (d >> 1)) & 3
        return x1, z1 * 8 + y1 * 2 + ((core + d) & 1)

    def data_copy(k):
        x1, t1 = there(k, 1)
        return pltpu.make_async_remote_copy(
            src_ref=send.at[x1 * plane + t1], dst_ref=recv.at[k], send_sem=data_out.at[k], recv_sem=data_in.at[k],
            device_id={"corr": x1, "tile": t1}, device_id_type=pl.DeviceIdType.MESH,
        )

    def start(k, carry):
        data_copy(k).start()
        return carry

    lax.fori_loop(1, devices, start, 0)
    recv[0] = send[corr * plane + tile]
    acc[...] = jnp.zeros_like(acc)

    line = lax.broadcasted_iota(jnp.int32, (NJ, LANES), 0)
    chosen = one_hot(lax.broadcasted_iota(jnp.int32, (NJ, LANES), 1) == tile * slots + line)
    shape = (2 * plane, plane * META)
    picked = lax.broadcasted_iota(jnp.int32, shape, 0)
    picked = (picked & (plane - 1)) * META + (picked >> 5) == lax.broadcasted_iota(jnp.int32, shape, 1)
    picked = one_hot(picked)
    for x in range(planes):
        lines = jnp.dot(picked, meta[x].reshape(plane * META, LANES), preferred_element_type=jnp.float32)
        part = lax.dot_general(
            chosen, lines.astype(jnp.bfloat16), (((1,), (1,)), ((), ())), preferred_element_type=jnp.float32
        )
        places_row[x] = jnp.concatenate([part, part], axis=1).astype(jnp.int32)
    scalars = pltpu.make_async_copy(places_row, places, own_sem)
    scalars.start()
    scalars.wait()

    lane = lax.broadcasted_iota(jnp.int32, (NJ, LANES), 1)
    batch = 4
    depth = batch * CAP * SUB
    target_lane = lax.broadcasted_iota(jnp.int32, (1, depth), 1)
    target_row = lax.broadcasted_iota(jnp.int32, (TILE_SIDE, depth), 0)

    def group(g, carry):
        firsts = [jnp.zeros((1, depth), jnp.int32) for _ in range(per_owner)]
        for i in range(batch):
            k = g * batch + i

            @pl.when(k > 0)
            def _():
                data_copy(k).wait()

            x1, t1 = there(k, -1)
            for slot in range(slots):
                row0, col0 = places[x1, slot, t1], places[x1, slot, plane + t1]
                begin = jnp.where(row0 >= 0, row0, 2 * LANES)
                inside = (lane >= begin) & (lane < begin + SUB)
                block = recv[k, slot * 2 * NJ:(slot + 1) * 2 * NJ].astype(jnp.float32)
                number = i * CAP + slot % CAP
                for part in range(2):
                    data = block[part * NJ:(part + 1) * NJ]
                    rolled = []
                    for a4 in range(4):
                        shift = (row0 + (LANES - a4 * SUB)) & (LANES - 1)
                        rolled.append(jnp.where(inside, pltpu.roll(data, shift, 1), 0.0))
                    rolled = jnp.concatenate(rolled, axis=0).astype(jnp.bfloat16)
                    moved[slot // CAP, number * SUB:(number + 1) * SUB, part * LANES:(part + 1) * LANES] = rolled
                firsts[slot // CAP] = jnp.where(target_lane >= number * SUB, col0 - number * SUB, firsts[slot // CAP])
        for own_tile in range(per_owner):
            select = one_hot(target_row == firsts[own_tile] + target_lane)
            acc[own_tile] += jnp.dot(select, moved[own_tile], preferred_element_type=jnp.float32)
        return carry

    lax.fori_loop(0, devices // batch, group, 0)
    for own_tile in range(per_owner):
        for part in range(2):
            out_ref[own_tile, part] = acc[own_tile, :, part * LANES:(part + 1) * LANES].T
    for number, unit in enumerate(sent):
        unit_copy(chip(core, unit[0], unit[1]), unit[2], pair, send_sems.at[number], pair_sems.at[0]).wait_send()


WAITS = (3, 4, 5, 6, 7, 9, 11, 13, None, None, None, None)
ORDER = 37
META = 16
PARTS = 2 * SUB // META


def per_device(visibilities, coords, stations, tile_ids, offsets, screens):
    planes, plane = lax.axis_size("corr"), lax.axis_size("tile")
    devices = planes * plane
    per_owner = NT // plane
    count = visibilities.shape[0]
    points = count * NCORR
    block = (devices, per_owner * CAP * 2 * NJ, LANES)
    vmem = pl.BlockSpec(memory_space=pltpu.VMEM)
    dma = pltpu.SemaphoreType.DMA
    return pl.pallas_call(
        functools.partial(grid_kernel, 4, WAITS, per_owner),
        out_shape=jax.ShapeDtypeStruct((per_owner, 2, TILE_SIDE, TILE_SIDE), jnp.float32),
        in_specs=[pl.BlockSpec(memory_space=pltpu.SMEM)] + [vmem] * 7,
        out_specs=vmem,
        scratch_shapes=[
            pltpu.VMEM((plane, screens.shape[0] * PARTS + 1, META, LANES), jnp.bfloat16),
            pltpu.VMEM((planes, plane, META, LANES), jnp.bfloat16),
            pltpu.VMEM((count, 2 * SUB, LANES), jnp.float32),
            pltpu.VMEM((points * NJ, LANES), jnp.float32),
            pltpu.VMEM((points * NJ, LANES), jnp.float32),
            pltpu.VMEM((NJ, points, 2 * LANES), jnp.bfloat16),
            pltpu.VMEM((points * NJ, LANES), jnp.float32),
            pltpu.VMEM((points * NJ, LANES), jnp.float32),
            pltpu.VMEM(block, jnp.bfloat16),
            pltpu.VMEM(block, jnp.bfloat16),
            pltpu.VMEM((per_owner, 4 * CAP * SUB, 2 * LANES), jnp.bfloat16),
            pltpu.VMEM((per_owner, TILE_SIDE, 2 * LANES), jnp.float32),
            pltpu.VMEM((1, NT * CAP), jnp.int32),
            pltpu.SMEM((1, NT * CAP), jnp.int32),
            pltpu.VMEM((planes, NJ, LANES), jnp.int32),
            pltpu.SMEM((planes, NJ, LANES), jnp.int32),
            dma((62,)),
            dma((32,)),
            dma((32,)),
            dma((planes,)),
            dma((planes,)),
            dma((devices,)),
            dma((devices,)),
            dma,
        ],
        compiler_params=pltpu.CompilerParams(vmem_limit_bytes=VMEM_LIMIT, collective_id=0, has_side_effects=True),
        name="grid",
    )(stations.T, screens, visibilities, coords.transpose(1, 0, 2), tile_ids.T, offsets.T, taper_table(), uv_tables())[None]


def solution(mesh):
    return jax.shard_map(
        per_device,
        mesh=mesh,
        in_specs=(
            P(("corr", "tile"), None, None),
            P(("corr", "tile"), None, None),
            P(("corr", "tile"), None),
            P(("corr", "tile"), None),
            P(("corr", "tile"), None),
            P("tile", None, None),
        ),
        out_specs=P("corr", "tile", None, None, None),
        check_vma=False,
    )
```

time: 153 us -> 80.9 us (0.53)
  waiting for transfers between devices: 65.2 us -> 0 us
  Pallas kernels: 42.7 us -> 79.1 us
  blocking collectives: 16.7 us -> 0 us
  between operations: 13.4 us -> 0.01 us
  local copies, waits for them, and re-layouts: 9.58 us -> 1.67 us
  starting transfers between devices: 4.62 us -> 0 us
    all_gather x1 -> x0, waiting for transfers between devices: 37 us -> none  [per_device(): all_screens = lax.all_gather(own, 'tile', axis=0, tiled=True)]
    pallas_call x3 -> x1, Pallas kernels: 42.7 us -> 79.1 us  [per_device(): pl.pallas_call(functools.partial(grid_kernel, 4, WAITS, per_owner), out_s...]
    all_to_all x1 -> x0, waiting for transfers between devices: 28.2 us -> none  [per_device(): lax.all_to_all(sending.reshape(NCORR * tile_size, rows, LANES), ('corr',...]
    all_to_all x1 -> x0, blocking collectives: 16.7 us -> none  [per_device(): lax.all_to_all(meta.reshape(corr_size * tile_size, per_owner * CAP), ('co...]
    all_to_all x1 -> x0, starting transfers between devices: 4.62 us -> none  [per_device(): lax.all_to_all(sending.reshape(NCORR * tile_size, rows, LANES), ('corr',...]
    unnamed x5 -> x1, local copies, waits for them, and re-layouts: 5.86 us -> 1.67 us
    reshape x2 -> x0, local copies, waits for them, and re-layouts: 2.44 us -> none  [the longest x1 1.76 us: per_device(): own = screens.reshape(screens.shape[0], 2 * SUB, LANES)]
  transfers between devices with their start and end apart: 2 -> 0, of which waited for: 2 -> 0; matrix products, arithmetic and copies ran while one was open for 4% -> 0% of each run, Pallas kernels for 11% -> 0%
where the time goes in v4:
time: 80.9 us; the launch traced here: 80.8 us
  Pallas kernels  79.1 us (98%)
  local copies, waits for them, and re-layouts  1.67 us (2%)
    pallas_call x1, Pallas kernels, per_device(): pl.pallas_call(functools.partial(grid_kernel, 4, WAITS, per_owner), out_s...  79.1 us
    unnamed x1, local copies, waits for them, and re-layouts  1.67 us

profile of v4, /device:TPU:1, one launch (start us, length us, event | category | flops | bytes accessed | tf_op | source)
XLA Modules:
  0.0 80.8 jit_solution(14438300501451420506)
XLA Ops:
  0.0 79.1 %grid.1 = f32[2,2,128,128]{3,2,1,0:T(8,128)} custom-call(s32[2,64]{1,0:T(2,128)} %bitcast.7, bf16[16,8,1024]{2,1,0:T(8,128)(2,1)} %own_ref.1, bf16[64,8,256]{2,1,0:T(8,128)(2,1)} %vis_ref.1, f32[3,64,256]{2,1,0:T(8,128)} %bitcast.6, s32[1,64]{1,0:T(1,128)} %bitcast.9, s32[2,64]{1,0:T(2,128)} %bitcast.8, f32[8,128]{1,0:T(8,128)} %constant.4.clone.taper_ref, ...), custom_call_target="tpu_custom_call" | custom-call | tf_op jit(solution)/shard_map/grid/pallas_call | solution.py:504
  79.1 1.7 %copy.10 = f32[1,2,2,128,128]{4,3,2,1,0:T(8,128)} copy(f32[1,2,2,128,128]{4,3,2,1,0:T(8,128)} %bitcast.5) | data formatting | bytes 524288

commit v5 on v4

--- a/solution.py
+++ b/solution.py
@@ -308,7 +308,7 @@
 
     first, second = direction_tables()
 
-    def compute(begin, end):
+    def compute(begin):
         def step(s, carry):
             u, v, w = (coords_ref[axis, pl.ds(s, 1)] for axis in range(3))
             image_re, image_im = image_of(u, v, w, vis_ref[s], first, second)
@@ -316,13 +316,14 @@
             image[s, SUB:2 * SUB] = image_im
             return carry
 
-        lax.fori_loop(begin, end, step, 0)
+        for q in range(per_chunk):
+            step(begin + q, 0)
 
     groups = ring_plan()
     chunks = count // per_chunk
 
     def chunk(i, carry):
-        compute(i * per_chunk, (i + 1) * per_chunk)
+        compute(i * per_chunk)
         for group, when in zip(groups, waits):
             if when is not None:
                 @pl.when(i == when)
@@ -345,15 +346,18 @@
             for h in range(2):
                 await_pair((a, b, h))
 
+    shape = (2 * plane, plane * META)
+    picked = lax.broadcasted_iota(jnp.int32, shape, 0)
+    picked = (picked & (plane - 1)) * META + (picked >> 5) == lax.broadcasted_iota(jnp.int32, shape, 1)
+    picked = one_hot(picked)
+    lines = jnp.dot(picked, shards[:, groups_owned].reshape(plane * META, LANES), preferred_element_type=jnp.float32)
+    meta[corr] = lines.astype(jnp.bfloat16)
+
     def axis_copy(t, whose):
         return pltpu.make_async_remote_copy(
-            src_ref=shards.at[:, groups_owned], dst_ref=meta.at[whose],
+            src_ref=meta.at[whose], dst_ref=meta.at[whose],
             send_sem=axis_out.at[t], recv_sem=axis_in.at[t], device_id=along(t), device_id_type=pl.DeviceIdType.MESH,
         )
-
-    for t in range(1, planes):
-        axis_copy(t, corr).start()
-    meta[corr] = shards[:, groups_owned]
 
     taper = taper_ref[...]
 
@@ -369,7 +373,11 @@
             x_im[rows] = out_im[e] * taper
         return carry
 
-    lax.fori_loop(0, count, sandwich, 0, unroll=2)
+    lead = count // 8
+    lax.fori_loop(0, lead, sandwich, 0, unroll=2)
+    for t in range(1, planes):
+        axis_copy(t, corr).start()
+    lax.fori_loop(lead, count, sandwich, 0, unroll=2)
     points = 16
 
     def transform(i, carry):
@@ -422,21 +430,14 @@
         data_copy(k).start()
         return carry
 
-    lax.fori_loop(1, devices, start, 0)
     recv[0] = send[corr * plane + tile]
     acc[...] = jnp.zeros_like(acc)
+    lax.fori_loop(1, devices, start, 0)
 
     line = lax.broadcasted_iota(jnp.int32, (NJ, LANES), 0)
     chosen = one_hot(lax.broadcasted_iota(jnp.int32, (NJ, LANES), 1) == tile * slots + line)
-    shape = (2 * plane, plane * META)
-    picked = lax.broadcasted_iota(jnp.int32, shape, 0)
-    picked = (picked & (plane - 1)) * META + (picked >> 5) == lax.broadcasted_iota(jnp.int32, shape, 1)
-    picked = one_hot(picked)
     for x in range(planes):
-        lines = jnp.dot(picked, meta[x].reshape(plane * META, LANES), preferred_element_type=jnp.float32)
-        part = lax.dot_general(
-            chosen, lines.astype(jnp.bfloat16), (((1,), (1,)), ((), ())), preferred_element_type=jnp.float32
-        )
+        part = lax.dot_general(chosen, meta[x], (((1,), (1,)), ((), ())), preferred_element_type=jnp.float32)
         places_row[x] = jnp.concatenate([part, part], axis=1).astype(jnp.int32)
     scalars = pltpu.make_async_copy(places_row, places, own_sem)
     scalars.start()
@@ -508,7 +509,7 @@
         out_specs=vmem,
         scratch_shapes=[
             pltpu.VMEM((plane, screens.shape[0] * PARTS + 1, META, LANES), jnp.bfloat16),
-            pltpu.VMEM((planes, plane, META, LANES), jnp.bfloat16),
+            pltpu.VMEM((planes, 2 * plane, LANES), jnp.bfloat16),
             pltpu.VMEM((count, 2 * SUB, LANES), jnp.float32),
             pltpu.VMEM((points * NJ, LANES), jnp.float32),
             pltpu.VMEM((points * NJ, LANES), jnp.float32),

time: 80.9 us -> 72.4 us (0.89)
  Pallas kernels: 79.1 us -> 70.6 us
    pallas_call x1, Pallas kernels: 79.1 us -> 70.6 us  [per_device(): pl.pallas_call(functools.partial(grid_kernel, 4, WAITS, per_owner), out_s...]
where the time goes in v5:
time: 72.4 us; the launch traced here: 72.2 us
  Pallas kernels  70.6 us (98%)
  local copies, waits for them, and re-layouts  1.67 us (2%)
    pallas_call x1, Pallas kernels, per_device(): pl.pallas_call(functools.partial(grid_kernel, 4, WAITS, per_owner), out_s...  70.6 us
    unnamed x1, local copies, waits for them, and re-layouts  1.67 us

profile of v5, /device:TPU:1, one launch (start us, length us, event | category | flops | bytes accessed | tf_op | source)
XLA Modules:
  0.0 72.2 jit_solution(598077385303732869)
XLA Ops:
  0.0 70.6 %grid.1 = f32[2,2,128,128]{3,2,1,0:T(8,128)} custom-call(s32[2,64]{1,0:T(2,128)} %bitcast.7, bf16[16,8,1024]{2,1,0:T(8,128)(2,1)} %own_ref.1, bf16[64,8,256]{2,1,0:T(8,128)(2,1)} %vis_ref.1, f32[3,64,256]{2,1,0:T(8,128)} %bitcast.6, s32[1,64]{1,0:T(1,128)} %bitcast.9, s32[2,64]{1,0:T(2,128)} %bitcast.8, f32[8,128]{1,0:T(8,128)} %constant.4.clone.taper_ref, ...), custom_call_target="tpu_custom_call" | custom-call | tf_op jit(solution)/shard_map/grid/pallas_call | solution.py:505
  70.6 1.7 %copy.10 = f32[1,2,2,128,128]{4,3,2,1,0:T(8,128)} copy(f32[1,2,2,128,128]{4,3,2,1,0:T(8,128)} %bitcast.5) | data formatting | bytes 524288

commit v6 on v5

--- a/solution.py
+++ b/solution.py
@@ -207,9 +207,9 @@
     return total(number), total(rows + 1) - 1, total(cols)
 
 
-def grid_kernel(per_chunk, waits, per_owner, stations, own_ref, vis_ref, coords_ref, tiles_ref, offsets_ref, taper_ref,
-                uv_ref, out_ref, shards, meta, image, x_re, x_im, y_ref, u_re, u_im, send, recv, moved, acc, order_row,
-                order, places_row, places, send_sems, ring_sems, pair_sems, axis_out, axis_in, data_out, data_in, own_sem):
+def grid_kernel(per_chunk, waits, per_owner, stations, own_ref, coords_ref, tiles_ref, offsets_ref, taper_ref,
+                uv_far, vis_far, out_ref, shards, meta, image, x_re, x_im, y_ref, u_re, u_im, send, recv, moved, acc, order_row,
+                order, places_row, places, send_sems, ring_sems, pair_sems, axis_out, axis_in, data_out, data_in, own_sem, uv_ref, vis_ref, uv_sem, vis_sem):
     corr, tile = lax.axis_index("corr"), lax.axis_index("tile")
     planes, plane = lax.axis_size("corr"), lax.axis_size("tile")
     devices = planes * plane
@@ -232,6 +232,10 @@
     def along(t):
         return {"corr": (corr + t) & (planes - 1)}
 
+    vis_load = pltpu.make_async_copy(vis_far, vis_ref, vis_sem)
+    vis_load.start()
+    uv_load = pltpu.make_async_copy(uv_far, uv_ref, uv_sem)
+    uv_load.start()
     barrier = pltpu.get_barrier_semaphore()
     for target in targets:
         pl.semaphore_signal(barrier, inc=1, device_id={"tile": target}, device_id_type=pl.DeviceIdType.MESH)
@@ -333,7 +337,9 @@
                         forward(unit)
         return carry
 
+    vis_load.wait()
     lax.fori_loop(0, chunks, chunk, 0)
+    uv_load.wait()
     scalars = pltpu.make_async_copy(order_row, order, own_sem)
     scalars.start()
     for group, when in zip(groups, waits):
@@ -505,7 +511,7 @@
     return pl.pallas_call(
         functools.partial(grid_kernel, 4, WAITS, per_owner),
         out_shape=jax.ShapeDtypeStruct((per_owner, 2, TILE_SIDE, TILE_SIDE), jnp.float32),
-        in_specs=[pl.BlockSpec(memory_space=pltpu.SMEM)] + [vmem] * 7,
+        in_specs=[pl.BlockSpec(memory_space=pltpu.SMEM)] + [vmem] * 5 + [pl.BlockSpec(memory_space=pl.ANY)] * 2,
         out_specs=vmem,
         scratch_shapes=[
             pltpu.VMEM((plane, screens.shape[0] * PARTS + 1, META, LANES), jnp.bfloat16),
@@ -532,10 +538,16 @@
             dma((devices,)),
             dma((devices,)),
             dma,
+            pltpu.VMEM((NJ, 2 * LANES, 2 * LANES), jnp.bfloat16),
+            pltpu.VMEM(visibilities.shape, visibilities.dtype),
+            dma,
+            dma,
         ],
         compiler_params=pltpu.CompilerParams(vmem_limit_bytes=VMEM_LIMIT, collective_id=0, has_side_effects=True),
         name="grid",
-    )(stations.T, screens, visibilities, coords.transpose(1, 0, 2), tile_ids.T, offsets.T, taper_table(), uv_tables())[None]
+    )(
+        stations.T, screens, coords.transpose(1, 0, 2), tile_ids.T, offsets.T, taper_table(), uv_tables(), visibilities
+    )[None]
 
 
 def solution(mesh):

time: 72.4 us -> 72 us (level)
  no operation moved by 1% of the time
where the time goes in v6:
time: 72 us; the launch traced here: 71.8 us
  Pallas kernels  70.1 us (97%)
  local copies, waits for them, and re-layouts  1.67 us (2%)
    pallas_call x1, Pallas kernels, per_device(): pl.pallas_call(functools.partial(grid_kernel, 4, WAITS, per_owner), out_s...  70.1 us
    unnamed x1, local copies, waits for them, and re-layouts  1.67 us

profile of v6, /device:TPU:1, one launch (start us, length us, event | category | flops | bytes accessed | tf_op | source)
XLA Modules:
  0.0 71.8 jit_solution(11233151029226258945)
XLA Ops:
  0.0 70.1 %grid.1 = f32[2,2,128,128]{3,2,1,0:T(8,128)} custom-call(s32[2,64]{1,0:T(2,128)} %bitcast.7, bf16[16,8,1024]{2,1,0:T(8,128)(2,1)} %own_ref.1, f32[3,64,256]{2,1,0:T(8,128)} %bitcast.6, s32[1,64]{1,0:T(1,128)} %bitcast.9, s32[2,64]{1,0:T(2,128)} %bitcast.8, f32[8,128]{1,0:T(8,128)} %constant.4.clone.taper_ref, bf16[8,256,256]{2,1,0:T(8,128)(2,1)} %constant.5.clone.uv_far, ...), custom_call_target="tpu_custom_call" | custom-call | tf_op jit(solution)/shard_map/grid/pallas_call | solution.py:511
  70.1 1.7 %copy.10 = f32[1,2,2,128,128]{4,3,2,1,0:T(8,128)} copy(f32[1,2,2,128,128]{4,3,2,1,0:T(8,128)} %bitcast.5) | data formatting | bytes 524288
